TPU v7x, 768 devices: a whole 4x8x12 slice. The times are simulated.
768 devices in a mesh: row: 16 (over x, y_hi, core), col: 48 (over y_lo, z).
Axes of the slice: x: 4, y: 8 (y_hi: 2, y_lo: 4; y = y_hi * 4 + y_lo), z: 12, core: 2. Of those that a mesh axis runs over, the one named last changes fastest.
Arguments:
- vectors: bfloat16 [16, 196608], P(None, ('row', 'col')), may hold values from -6 to 6
- tiles: bfloat16 [98304, 128, 128], P(('row', 'col')), may hold values from -0.046875 to 0.046875
- tile_rows: int32 [98304], P(('row', 'col')), may hold values from 0 to 95
- tile_cols: int32 [98304], P(('row', 'col')), may hold values from 0 to 95
- tile_count: int32 [768], P(('row', 'col')), may hold values from 32 to 128, as said below
Outputs:
- applied: float32 [16, 196608], P(None, ('row', 'col'))
Inputs may be any that keep to these rules, and one draw needn't show every extreme that they name: `tile_count`: each device has between 32 and 128 live slots; some device fills all 128.
All inputs are finite; a program needn't handle non-finite values.
Results may differ from a plain program's by a relative error of at most 0.0003.
Values may be sent and summed in bfloat16 or wider, within the bound.
No kernel may reach another device: no remote copies, remote signals or barrier semaphores. Data moves between devices by JAX's collectives and lax.ppermute only.
A program may use at most 32 MiB of HBM per device.

v0:
```python
import functools

import jax
import jax.numpy as jnp
from jax import lax
from jax.experimental import pallas as pl
from jax.experimental.pallas import tpu as pltpu
from jax.sharding import Mesh, PartitionSpec as P

CHUNK = 16
TOP = 14
ALL = ("rr", "core", "j", "m")


def vmem():
    return pl.BlockSpec(memory_space=pltpu.VMEM)


def powers(exponent):
    low = exponent >> 1
    return (
        jnp.exp2(low.astype(jnp.float32)),
        jnp.exp2((exponent - low).astype(jnp.float32)),
    )


def pack(left, right, payload, p):
    rows, width = left.shape
    half = rows // 2
    peak = jnp.max(jnp.maximum(jnp.abs(left), jnp.abs(right)), axis=1, keepdims=True)
    peak = jnp.maximum(peak, 1.2e-38)
    exponent = jnp.floor(jnp.log2(peak)).astype(jnp.int32)
    first, second = powers(TOP - exponent)
    for s, part in enumerate((left, right)):
        scaled = jnp.round((part * first) * second)
        scaled = jnp.minimum(jnp.maximum(scaled, -32767.0), 32767.0)
        payload[p, s * rows : (s + 1) * rows] = scaled.astype(jnp.int32).astype(jnp.int16)
    lane = lax.broadcasted_iota(jnp.int32, (half, width), 1)
    both = jnp.where(lane < width // 2, exponent[:half], exponent[half:])
    payload[p, 2 * rows : 2 * rows + half] = both.astype(jnp.int16)


def unpack(payload, p, rows):
    half = rows // 2
    width = payload.shape[-1]
    exponent = payload[p, 2 * rows : 2 * rows + half].astype(jnp.int32) - TOP
    first, second = powers(exponent)

    def spread_out(factor):
        upper = jnp.broadcast_to(factor[:, :1], (half, width))
        lower = jnp.broadcast_to(factor[:, width // 2 : width // 2 + 1], (half, width))
        return jnp.concatenate([upper, lower], axis=0)

    first, second = spread_out(first), spread_out(second)
    return [
        (payload[p, s * rows : (s + 1) * rows].astype(jnp.float32) * first) * second
        for s in range(2)
    ]


def product_kernel(mirror, meta, sources, targets, *refs):
    if mirror:
        own, tiles, keep, give, x, acc, held, sems = refs
        parts = [own]
    else:
        mine, theirs, tiles, payload, x, acc, held, sems = refs
        parts = [mine, theirs]
    slots, width = tiles.shape[0], tiles.shape[1]
    chunks = slots // CHUNK

    def copy(step):
        part = pl.ds(step * CHUNK, CHUNK)
        return pltpu.make_async_copy(tiles.at[part], held.at[part], sems.at[step])

    for step in range(chunks):
        copy(step).start()
    at = 0
    for part in parts:
        size = part.shape[0]
        for s in range(2):
            x[at : at + size, s] = part[:, :, s * width : (s + 1) * width]
        at += size
    x[at] = jnp.zeros(x.shape[1:], x.dtype)
    acc[...] = jnp.zeros_like(acc)
    count = meta[0]

    def step_body(step, carry):
        copy(step).wait()

        @pl.when(step * CHUNK < count)
        def _():
            found = []
            for u in range(CHUNK):
                k = step * CHUNK + u
                source = sources[k]
                found.append(
                    lax.dot_general(
                        x[source // 2, source % 2],
                        held[k],
                        (((1,), (0 if mirror else 1,)), ((), ())),
                        preferred_element_type=jnp.float32,
                    )
                )
            for u in range(CHUNK):
                target = targets[step * CHUNK + u]
                acc[target // 2, target % 2] += found[u]

        return carry

    lax.fori_loop(0, chunks, step_body, 0)
    if mirror:
        half = keep.shape[0]
        keep[...] = acc[:half]
        give[...] = acc[half:]
    else:

        def pack_body(p, carry):
            pack(acc[p, 0], acc[p, 1], payload, p)
            return carry

        lax.fori_loop(0, payload.shape[0], pack_body, 0, unroll=4)


def products(mirror, meta, sources, targets, segment, tiles):
    smem = pl.BlockSpec(memory_space=pltpu.SMEM)
    pieces = segment[0].shape[0] * len(segment)
    vecs = segment[0].shape[1]
    slots, width = tiles.shape[:2]
    if mirror:
        shapes = [jax.ShapeDtypeStruct((pieces // 2, 2, vecs, width), jnp.float32)] * 2
        outs = [vmem(), vmem()]
    else:
        shapes = jax.ShapeDtypeStruct((pieces, 5 * vecs // 2, width), jnp.int16)
        outs = vmem()
    return pl.pallas_call(
        functools.partial(product_kernel, mirror),
        out_shape=shapes,
        in_specs=[smem] * 3 + [vmem()] * len(segment) + [pl.BlockSpec(memory_space=pl.ANY)],
        out_specs=outs,
        scratch_shapes=[
            pltpu.VMEM((pieces + 1, 2, vecs, width), jnp.bfloat16),
            pltpu.VMEM((pieces, 2, vecs, width), jnp.float32),
            pltpu.VMEM((slots, width, width), jnp.bfloat16),
            pltpu.SemaphoreType.DMA((slots // CHUNK,)),
        ],
    )(meta, sources, targets, *segment, tiles)


def join_kernel(keep, came, payload):
    def body(p, carry):
        pack(keep[p, 0] + came[p, 0], keep[p, 1] + came[p, 1], payload, p)
        return carry

    lax.fori_loop(0, payload.shape[0], body, 0, unroll=4)


def join(keep, came):
    pieces, _, vecs, width = keep.shape
    return pl.pallas_call(
        join_kernel,
        out_shape=jax.ShapeDtypeStruct((pieces, 5 * vecs // 2, width), jnp.int16),
        in_specs=[vmem()] * 2,
        out_specs=vmem(),
    )(keep, came)


def total_kernel(kinds, vecs, payload, *refs):
    *added, out = refs
    width = payload.shape[-1]

    for kind in range(kinds):

        def body(i, sums, kind=kind):
            left, right = unpack(payload, i * kinds + kind, vecs)
            return sums[0] + left, sums[1] + right

        zero = jnp.zeros((vecs, width), jnp.float32)
        sums = lax.fori_loop(0, payload.shape[0] // kinds, body, (zero, zero), unroll=4)
        for s in range(2):
            lanes = slice(s * width, (s + 1) * width)
            total = sums[s]
            for other in added:
                total = total + other[:, lanes]
            out[kind, :, lanes] = total


def total(kinds, vecs, payload, *added):
    width = payload.shape[-1]
    return pl.pallas_call(
        functools.partial(total_kernel, kinds, vecs),
        out_shape=jax.ShapeDtypeStruct((kinds, vecs, 2 * width), jnp.float32),
        in_specs=[vmem()] * (1 + len(added)),
        out_specs=vmem(),
    )(payload, *added)


def spread(array, axes):
    size = lax.axis_size(axes)
    return lax.all_to_all(
        jnp.broadcast_to(array[None], (size, *array.shape)), axes, 0, 0, tiled=True
    )


def shards(vectors, tiles, tile_rows, tile_cols, tile_count):
    n_row, fold = lax.axis_size("m"), lax.axis_size("j")
    vecs = vectors.shape[0]
    slots = tiles.shape[0]
    row_index = lax.axis_index(("rr", "core"))
    core, j = lax.axis_index("core"), lax.axis_index("j")
    mirror_index = lax.axis_index("m")
    swap = [(0, 1), (1, 0)]
    shift = lambda k: [(i, (i + k) % fold) for i in range(fold)]
    turn = [
        ((r * fold + i) * n_row + a, (a * fold + i) * n_row + r)
        for r in range(n_row)
        for i in range(fold)
        for a in range(n_row)
    ]

    shard, half = tile_cols // 2, tile_cols % 2
    member = shard % n_row
    behind = (j - shard // n_row) % fold
    place = ((member % 2) ^ core) * (n_row // 2) + member // 2
    col_place = (place * fold + behind) * 2 + half
    nothing = 2 * n_row * fold
    live = jnp.arange(slots, dtype=jnp.int32) < tile_count[0]
    mirrored = live & ((row_index != mirror_index) | (tile_rows != tile_cols))
    mirror_source = jnp.where(mirrored, tile_rows, nothing)
    plain_source = jnp.where(live, col_place, nothing)

    own = spread(vectors, ("j", "m"))
    trio = jnp.stack([vectors] + [lax.ppermute(vectors, "j", shift(k)) for k in range(1, fold)])
    trio = lax.ppermute(trio, ALL, turn)
    own, trio = lax.optimization_barrier((own, trio))
    mine = spread(trio, "rr").reshape(-1, *vectors.shape)
    theirs = lax.ppermute(mine, "core", swap)

    keep, give = products(True, tile_count, mirror_source, col_place, [own], tiles)
    sums = join(keep, lax.ppermute(give, "core", swap))
    sums = lax.all_to_all(sums, "rr", 0, 0, tiled=True)
    sums = lax.ppermute(total(fold, vecs, sums), ALL, turn)
    mirror_sums = [sums[0]] + [lax.ppermute(sums[k], "j", shift(-k)) for k in range(1, fold)]

    plain = products(False, tile_count, plain_source, tile_rows, [mine, theirs], tiles)
    plain = lax.all_to_all(plain, ("j", "m"), 0, 0, tiled=True)
    return total(1, vecs, plain, *mirror_sums)[0]


def solution(mesh):
    n_row, n_col = mesh.shape["row"], mesh.shape["col"]
    fine = Mesh(mesh.devices.reshape(n_row // 2, 2, n_col // n_row, n_row), ALL)

    return jax.shard_map(
        shards,
        mesh=fine,
        in_specs=(P(None, ALL), P(ALL, None, None), P(ALL), P(ALL), P(ALL)),
        out_specs=P(None, ALL),
        check_vma=False,
    )
```

profile of v0, /device:TPU:138, one launch (start us, length us, event | category | flops | bytes accessed | tf_op | source)
XLA Modules:
  0.0 157.3 jit_solution(11305476387454438292)
XLA Ops:
  0.0 1.5 broadcast_in_dim.20
  1.5 17.2 %all-to-all-start = ((bf16[48,16,256]{2,1,0:T(8,128)(2,1)}), bf16[48,16,256]{2,1,0:T(8,128)(2,1)S(1)}, u32[]{:S(2)}, u32[]{:S(2)}) async-start(bf16[48,16,256]{2,1,0:T(8,128)(2,1)} %broadcast_in_dim.20), calls=%async_computation | async-start | bytes 786432 | tf_op jit(solution)/shard_map/all_to_all | solution.py:199
  18.6 8.3 %collective-permute-start = (bf16[16,256]{1,0:T(8,128)(2,1)}, bf16[16,256]{1,0:T(8,128)(2,1)S(1)}, u32[]{:S(2)}, u32[]{:S(2)}) collective-permute-start(bf16[16,256]{1,0:T(8,128)(2,1)} %param.5), channel_id=1, source_target_pairs={{0,16},{16,32},{32,0},{1,17},{17,33},{33,1},{2,18},{18,34},{34,2},... | collective-permute-start | bytes 24584 | tf_op jit(solution)/shard_map/ppermute | solution.py:232
  26.9 3.3 %collective-permute-start.1 = (bf16[16,256]{1,0:T(8,128)(2,1)}, bf16[16,256]{1,0:T(8,128)(2,1)S(1)}, u32[]{:S(2)}, u32[]{:S(2)}) collective-permute-start(bf16[16,256]{1,0:T(8,128)(2,1)} %param.5), channel_id=1, source_target_pairs={{0,32},{16,0},{32,16},{1,33},{17,1},{33,17},{2,34},{18,2},{34,18},... | collective-permute-start | bytes 24584 | tf_op jit(solution)/shard_map/ppermute | solution.py:232
  30.9 5.0 %collective-permute-done = bf16[16,256]{1,0:T(8,128)(2,1)S(1)} collective-permute-done((bf16[16,256]{1,0:T(8,128)(2,1)}, bf16[16,256]{1,0:T(8,128)(2,1)S(1)}, u32[]{:S(2)}, u32[]{:S(2)}) %collective-permute-start) | collective-permute-done | bytes 8224 | tf_op jit(solution)/shard_map/ppermute | solution.py:232
  35.8 1.9 %collective-permute-done.1 = bf16[16,256]{1,0:T(8,128)(2,1)S(1)} collective-permute-done((bf16[16,256]{1,0:T(8,128)(2,1)}, bf16[16,256]{1,0:T(8,128)(2,1)S(1)}, u32[]{:S(2)}, u32[]{:S(2)}) %collective-permute-start.1) | collective-permute-done | bytes 8224 | tf_op jit(solution)/shard_map/ppermute | solution.py:232
  37.7 0.7 pad_maximum_fusion
  38.5 6.8 %collective-permute-start.2 = (bf16[3,16,256]{2,1,0:T(8,128)(2,1)S(1)}, bf16[3,16,256]{2,1,0:T(8,128)(2,1)S(1)}, u32[]{:S(2)}, u32[]{:S(2)}) collective-permute-start(bf16[3,16,256]{2,1,0:T(8,128)(2,1)S(1)} %pad_maximum_fusion), channel_id=1, source_target_pairs={{0,0},{1,48},{2,96},{3,144},{4,192},{5,240},{6,288},{7,336},{8,384... | collective-permute-start | bytes 73736 | tf_op jit(solution)/shard_map/ppermute | solution.py:233
  45.3 1.3 compare_select_fusion.9
  46.6 7.9 %collective-permute-done.2 = bf16[3,16,256]{2,1,0:T(8,128)(2,1)S(1)} collective-permute-done((bf16[3,16,256]{2,1,0:T(8,128)(2,1)S(1)}, bf16[3,16,256]{2,1,0:T(8,128)(2,1)S(1)}, u32[]{:S(2)}, u32[]{:S(2)}) %collective-permute-start.2) | collective-permute-done | bytes 24608 | tf_op jit(solution)/shard_map/ppermute | solution.py:233
  54.4 0.0 all-to-all-done.refs_0_
  54.4 0.0 copy-start.1
  54.4 0.8 copy-done.1
  55.2 4.1 %shard_map.56 = (f32[24,2,16,128]{3,2,1,0:T(8,128)}, f32[24,2,16,128]{3,2,1,0:T(8,128)}) custom-call(s32[1]{0:T(128)} %copy.6.meta, s32[128]{0:T(128)} %get-tuple-element.18.sources, s32[128]{0:T(128)} %get-tuple-element.14.targets, bf16[48,16,256]{2,1,0:T(8,128)(2,1)} %copy-done.1, bf16[128,128,128]{2,1,0:T(8,128)(2,1)} %refs_1_.1), custom_call_target="tpu_custom_call" | custom-call | tf_op jit(solution)/shard_map/pallas_call | solution.py:135
  59.4 1.9 %collective-permute-start.4 = (f32[24,2,16,128]{3,2,1,0:T(8,128)}, f32[24,2,16,128]{3,2,1,0:T(8,128)S(1)}, u32[]{:S(2)}, u32[]{:S(2)}) collective-permute-start(f32[24,2,16,128]{3,2,1,0:T(8,128)} %get-tuple-element.12), channel_id=1, source_target_pairs={{0,48},{48,0},{1,49},{49,1},{2,50},{50,2},{3,51},{51,3},{4,52},{52... | collective-permute-start | bytes 1179656 | tf_op jit(solution)/shard_map/ppermute | solution.py:239
  61.3 0.7 broadcast_in_dim.22
  62.0 6.2 %all-to-all-start.1 = ((bf16[8,3,16,256]{3,2,1,0:T(8,128)(2,1)}), bf16[8,3,16,256]{3,2,1,0:T(8,128)(2,1)S(1)}, u32[]{:S(2)}, u32[]{:S(2)}) async-start(bf16[8,3,16,256]{3,2,1,0:T(8,128)(2,1)} %broadcast_in_dim.22), calls=%async_computation.1 | async-start | bytes 393216 | tf_op jit(solution)/shard_map/all_to_all | solution.py:199
  68.1 0.0 collective-permute-done.4.came
  68.1 0.0 copy-start.4
  68.1 0.7 copy-done.4
  68.9 2.5 %shard_map.57 = s16[24,40,128]{2,1,0:T(8,128)(2,1)} custom-call(f32[24,2,16,128]{3,2,1,0:T(8,128)} %get-tuple-element.11.keep, f32[24,2,16,128]{3,2,1,0:T(8,128)} %copy-done.4), custom_call_target="tpu_custom_call" | custom-call | tf_op jit(solution)/shard_map/pallas_call | solution.py:159
  71.4 6.3 %all-to-all-done.1 = bf16[8,3,16,256]{3,2,1,0:T(8,128)(2,1)S(1)} async-done(((bf16[8,3,16,256]{3,2,1,0:T(8,128)(2,1)}), bf16[8,3,16,256]{3,2,1,0:T(8,128)(2,1)S(1)}, u32[]{:S(2)}, u32[]{:S(2)}) %all-to-all-start.1) | async-done | bytes 196640 | tf_op jit(solution)/shard_map/all_to_all | solution.py:199
  77.7 0.0 copy-start.3
  77.7 5.0 %all-to-all-start.3 = ((s16[24,40,128]{2,1,0:T(8,128)(2,1)}), s16[24,40,128]{2,1,0:T(8,128)(2,1)S(1)}, u32[]{:S(2)}, u32[]{:S(2)}) async-start(s16[24,40,128]{2,1,0:T(8,128)(2,1)} %shard_map.57), calls=%async_computation.3 | async-start | bytes 491520 | tf_op jit(solution)/shard_map/all_to_all | solution.py:240
  82.7 1.9 %collective-permute-start.3 = (bf16[24,16,256]{2,1,0:T(8,128)(2,1)S(1)}, bf16[24,16,256]{2,1,0:T(8,128)(2,1)S(1)}, u32[]{:S(2)}, u32[]{:S(2)}) collective-permute-start(bf16[24,16,256]{2,1,0:T(8,128)(2,1)S(1)} %bitcast.13), channel_id=1, source_target_pairs={{0,48},{48,0},{1,49},{49,1},{2,50},{50,2},{3,51},{51,3},{4,52},{52... | collective-permute-start | bytes 589832 | tf_op jit(solution)/shard_map/ppermute | solution.py:236
  84.6 1.4 collective-permute-done.3.refs_1_
  86.0 0.0 copy-start.5
  86.0 0.0 copy-done.3
  86.0 0.7 copy-done.5
  86.7 5.9 %shard_map.55 = s16[48,40,128]{2,1,0:T(8,128)(2,1)} custom-call(s32[1]{0:T(128)} %copy.6.meta, s32[128]{0:T(128)} %get-tuple-element.13.sources, s32[128]{0:T(128)} %targets.1, bf16[24,16,256]{2,1,0:T(8,128)(2,1)} %bitcast.14, bf16[24,16,256]{2,1,0:T(8,128)(2,1)} %copy-done.5, bf16[128,128,128]{2,1,0:T(8,128)(2,1)} %refs_1_.1), custom_call_target="tpu_custom_call" | custom-call | tf_op jit(solution)/shard_map/pallas_call | solution.py:135
  92.6 0.0 all-to-all-done.3.payload
  92.7 0.0 copy-start.2
  92.7 12.5 %all-to-all-start.2 = ((s16[48,40,128]{2,1,0:T(8,128)(2,1)}), s16[48,40,128]{2,1,0:T(8,128)(2,1)S(1)}, u32[]{:S(2)}, u32[]{:S(2)}) async-start(s16[48,40,128]{2,1,0:T(8,128)(2,1)} %shard_map.55), calls=%async_computation.2 | async-start | bytes 983040 | tf_op jit(solution)/shard_map/all_to_all | solution.py:245
  105.2 0.0 copy-done.2
  105.2 2.1 %shard_map.58 = f32[3,16,256]{2,1,0:T(8,128)} custom-call(s16[24,40,128]{2,1,0:T(8,128)(2,1)} %copy-done.2), custom_call_target="tpu_custom_call" | custom-call | tf_op jit(solution)/shard_map/pallas_call | solution.py:189
  107.4 10.7 %collective-permute-start.5 = (f32[3,16,256]{2,1,0:T(8,128)}, f32[3,16,256]{2,1,0:T(8,128)S(1)}, u32[]{:S(2)}, u32[]{:S(2)}) collective-permute-start(f32[3,16,256]{2,1,0:T(8,128)} %shard_map.58), channel_id=1, source_target_pairs={{0,0},{1,48},{2,96},{3,144},{4,192},{5,240},{6,288},{7,336},{8,384... | collective-permute-start | bytes 147464 | tf_op jit(solution)/shard_map/ppermute | solution.py:241
  118.1 18.2 %collective-permute-done.5 = f32[3,16,256]{2,1,0:T(8,128)S(1)} collective-permute-done((f32[3,16,256]{2,1,0:T(8,128)}, f32[3,16,256]{2,1,0:T(8,128)S(1)}, u32[]{:S(2)}, u32[]{:S(2)}) %collective-permute-start.5) | collective-permute-done | bytes 49184 | tf_op jit(solution)/shard_map/ppermute | solution.py:241
  136.3 0.6 slice_bitcast_fusion
  136.9 5.4 %collective-permute-start.6 = (f32[16,256]{1,0:T(8,128)S(1)}, f32[16,256]{1,0:T(8,128)S(1)}, u32[]{:S(2)}, u32[]{:S(2)}) collective-permute-start(f32[16,256]{1,0:T(8,128)S(1)} %get-tuple-element.16), channel_id=1, source_target_pairs={{0,32},{16,0},{32,16},{1,33},{17,1},{33,17},{2,34},{18,2},{34,18},... | collective-permute-start | bytes 49160 | tf_op jit(solution)/shard_map/ppermute | solution.py:242
  142.3 5.2 %collective-permute-start.7 = (f32[16,256]{1,0:T(8,128)S(1)}, f32[16,256]{1,0:T(8,128)S(1)}, u32[]{:S(2)}, u32[]{:S(2)}) collective-permute-start(f32[16,256]{1,0:T(8,128)S(1)} %get-tuple-element.15), channel_id=1, source_target_pairs={{0,16},{16,32},{32,0},{1,17},{17,33},{33,1},{2,18},{18,34},{34,2},... | collective-permute-start | bytes 49160 | tf_op jit(solution)/shard_map/ppermute | solution.py:242
  147.6 0.0 collective-permute-done.6.refs_1_
  147.6 0.0 copy-start.6
  147.6 6.1 %collective-permute-done.7.refs_2_ = f32[16,256]{1,0:T(8,128)S(1)} collective-permute-done((f32[16,256]{1,0:T(8,128)S(1)}, f32[16,256]{1,0:T(8,128)S(1)}, u32[]{:S(2)}, u32[]{:S(2)}) %collective-permute-start.7) | collective-permute-done | bytes 16416 | tf_op jit(solution)/shard_map/ppermute | solution.py:242
  153.6 0.0 copy-start.7
  153.6 0.0 all-to-all-done.2.payload
  153.7 0.0 copy-start
  153.7 0.0 copy-done.6
  153.7 0.6 copy-done.7
  154.2 0.2 copy-done
  154.5 2.8 %shard_map.59 = f32[1,16,256]{2,1,0:T(8,128)} custom-call(s16[48,40,128]{2,1,0:T(8,128)(2,1)} %copy-done, f32[16,256]{1,0:T(8,128)} %get-tuple-element.17.refs_0_, f32[16,256]{1,0:T(8,128)} %copy-done.6, f32[16,256]{1,0:T(8,128)} %copy-done.7), custom_call_target="tpu_custom_call" | custom-call | tf_op jit(solution)/shard_map/pallas_call | solution.py:189
Async XLA Ops:
  1.5 53.0 %all-to-all-start = ((bf16[48,16,256]{2,1,0:T(8,128)(2,1)}), bf16[48,16,256]{2,1,0:T(8,128)(2,1)S(1)}, u32[]{:S(2)}, u32[]{:S(2)}) async-start(bf16[48,16,256]{2,1,0:T(8,128)(2,1)} %broadcast_in_dim.20), calls=%async_computation | async-start | bytes 786432 | tf_op jit(solution)/shard_map/all_to_all | solution.py:199
  18.6 17.2 %collective-permute-start = (bf16[16,256]{1,0:T(8,128)(2,1)}, bf16[16,256]{1,0:T(8,128)(2,1)S(1)}, u32[]{:S(2)}, u32[]{:S(2)}) collective-permute-start(bf16[16,256]{1,0:T(8,128)(2,1)} %param.5), channel_id=1, source_target_pairs={{0,16},{16,32},{32,0},{1,17},{17,33},{33,1},{2,18},{18,34},{34,2},... | collective-permute-start | bytes 24584 | tf_op jit(solution)/shard_map/ppermute | solution.py:232
  26.9 10.8 %collective-permute-start.1 = (bf16[16,256]{1,0:T(8,128)(2,1)}, bf16[16,256]{1,0:T(8,128)(2,1)S(1)}, u32[]{:S(2)}, u32[]{:S(2)}) collective-permute-start(bf16[16,256]{1,0:T(8,128)(2,1)} %param.5), channel_id=1, source_target_pairs={{0,32},{16,0},{32,16},{1,33},{17,1},{33,17},{2,34},{18,2},{34,18},... | collective-permute-start | bytes 24584 | tf_op jit(solution)/shard_map/ppermute | solution.py:232
  38.5 16.0 %collective-permute-start.2 = (bf16[3,16,256]{2,1,0:T(8,128)(2,1)S(1)}, bf16[3,16,256]{2,1,0:T(8,128)(2,1)S(1)}, u32[]{:S(2)}, u32[]{:S(2)}) collective-permute-start(bf16[3,16,256]{2,1,0:T(8,128)(2,1)S(1)} %pad_maximum_fusion), channel_id=1, source_target_pairs={{0,0},{1,48},{2,96},{3,144},{4,192},{5,240},{6,288},{7,336},{8,384... | collective-permute-start | bytes 73736 | tf_op jit(solution)/shard_map/ppermute | solution.py:233
  54.4 0.8 copy-start.1
  59.4 8.8 %collective-permute-start.4 = (f32[24,2,16,128]{3,2,1,0:T(8,128)}, f32[24,2,16,128]{3,2,1,0:T(8,128)S(1)}, u32[]{:S(2)}, u32[]{:S(2)}) collective-permute-start(f32[24,2,16,128]{3,2,1,0:T(8,128)} %get-tuple-element.12), channel_id=1, source_target_pairs={{0,48},{48,0},{1,49},{49,1},{2,50},{50,2},{3,51},{51,3},{4,52},{52... | collective-permute-start | bytes 1179656 | tf_op jit(solution)/shard_map/ppermute | solution.py:239
  62.0 15.7 %all-to-all-start.1 = ((bf16[8,3,16,256]{3,2,1,0:T(8,128)(2,1)}), bf16[8,3,16,256]{3,2,1,0:T(8,128)(2,1)S(1)}, u32[]{:S(2)}, u32[]{:S(2)}) async-start(bf16[8,3,16,256]{3,2,1,0:T(8,128)(2,1)} %broadcast_in_dim.22), calls=%async_computation.1 | async-start | bytes 393216 | tf_op jit(solution)/shard_map/all_to_all | solution.py:199
  68.1 0.7 copy-start.4
  77.7 8.4 %copy-start.3 = (bf16[8,3,16,256]{3,2,1,0:T(8,128)(2,1)}, bf16[8,3,16,256]{3,2,1,0:T(8,128)(2,1)S(1)}, u32[]{:S(2)}) copy-start(bf16[8,3,16,256]{3,2,1,0:T(8,128)(2,1)S(1)} %all-to-all-done.1) | copy-start | bytes 589828
  77.7 15.0 %all-to-all-start.3 = ((s16[24,40,128]{2,1,0:T(8,128)(2,1)}), s16[24,40,128]{2,1,0:T(8,128)(2,1)S(1)}, u32[]{:S(2)}, u32[]{:S(2)}) async-start(s16[24,40,128]{2,1,0:T(8,128)(2,1)} %shard_map.57), calls=%async_computation.3 | async-start | bytes 491520 | tf_op jit(solution)/shard_map/all_to_all | solution.py:240
  82.7 3.3 %collective-permute-start.3 = (bf16[24,16,256]{2,1,0:T(8,128)(2,1)S(1)}, bf16[24,16,256]{2,1,0:T(8,128)(2,1)S(1)}, u32[]{:S(2)}, u32[]{:S(2)}) collective-permute-start(bf16[24,16,256]{2,1,0:T(8,128)(2,1)S(1)} %bitcast.13), channel_id=1, source_target_pairs={{0,48},{48,0},{1,49},{49,1},{2,50},{50,2},{3,51},{51,3},{4,52},{52... | collective-permute-start | bytes 589832 | tf_op jit(solution)/shard_map/ppermute | solution.py:236
  86.0 0.7 copy-start.5
  92.7 12.6 %copy-start.2 = (s16[24,40,128]{2,1,0:T(8,128)(2,1)}, s16[24,40,128]{2,1,0:T(8,128)(2,1)S(1)}, u32[]{:S(2)}) copy-start(s16[24,40,128]{2,1,0:T(8,128)(2,1)S(1)} %all-to-all-done.3.payload) | copy-start | bytes 737284
  92.7 61.0 %all-to-all-start.2 = ((s16[48,40,128]{2,1,0:T(8,128)(2,1)}), s16[48,40,128]{2,1,0:T(8,128)(2,1)S(1)}, u32[]{:S(2)}, u32[]{:S(2)}) async-start(s16[48,40,128]{2,1,0:T(8,128)(2,1)} %shard_map.55), calls=%async_computation.2 | async-start | bytes 983040 | tf_op jit(solution)/shard_map/all_to_all | solution.py:245
  107.4 28.9 %collective-permute-start.5 = (f32[3,16,256]{2,1,0:T(8,128)}, f32[3,16,256]{2,1,0:T(8,128)S(1)}, u32[]{:S(2)}, u32[]{:S(2)}) collective-permute-start(f32[3,16,256]{2,1,0:T(8,128)} %shard_map.58), channel_id=1, source_target_pairs={{0,0},{1,48},{2,96},{3,144},{4,192},{5,240},{6,288},{7,336},{8,384... | collective-permute-start | bytes 147464 | tf_op jit(solution)/shard_map/ppermute | solution.py:241
  136.9 10.7 %collective-permute-start.6 = (f32[16,256]{1,0:T(8,128)S(1)}, f32[16,256]{1,0:T(8,128)S(1)}, u32[]{:S(2)}, u32[]{:S(2)}) collective-permute-start(f32[16,256]{1,0:T(8,128)S(1)} %get-tuple-element.16), channel_id=1, source_target_pairs={{0,32},{16,0},{32,16},{1,33},{17,1},{33,17},{2,34},{18,2},{34,18},... | collective-permute-start | bytes 49160 | tf_op jit(solution)/shard_map/ppermute | solution.py:242
  142.3 11.3 %collective-permute-start.7 = (f32[16,256]{1,0:T(8,128)S(1)}, f32[16,256]{1,0:T(8,128)S(1)}, u32[]{:S(2)}, u32[]{:S(2)}) collective-permute-start(f32[16,256]{1,0:T(8,128)S(1)} %get-tuple-element.15), channel_id=1, source_target_pairs={{0,16},{16,32},{32,0},{1,17},{17,33},{33,1},{2,18},{18,34},{34,2},... | collective-permute-start | bytes 49160 | tf_op jit(solution)/shard_map/ppermute | solution.py:242
  147.6 6.1 %copy-start.6 = (f32[16,256]{1,0:T(8,128)}, f32[16,256]{1,0:T(8,128)S(1)}, u32[]{:S(2)}) copy-start(f32[16,256]{1,0:T(8,128)S(1)} %collective-permute-done.6.refs_1_) | copy-start | bytes 49156
  153.6 0.6 copy-start.7
  153.7 0.8 copy-start
where the time goes:
time: 158 us; the launch traced here: 157 us
  starting transfers between devices  84.4 us (53%)
  waiting for transfers between devices  46.7 us (30%)
  Pallas kernels  17.6 us (11%)
  local copies, waits for them, and re-layouts  5.72 us (4%)
  other arithmetic  1.99 us (1%)
    all_to_all x2, starting transfers between devices, spread(): lax.all_to_all(jnp.broadcast_to(array[None], (size, *array.shape)), axes,...  23.3 us
    ppermute x1, waiting for transfers between devices, shards(): sums = lax.ppermute(total(fold, vecs, sums), ALL, turn)  18.2 us
    all_to_all x1, starting transfers between devices, shards(): plain = lax.all_to_all(plain, ('j', 'm'), 0, 0, tiled=True)  12.5 us
    ppermute x2, starting transfers between devices, shards(): lax.ppermute(vectors, 'j', shift(k))  11.6 us
    ppermute x1, starting transfers between devices, shards(): sums = lax.ppermute(total(fold, vecs, sums), ALL, turn)  10.7 us
    ppermute x2, starting transfers between devices, shards(): lax.ppermute(sums[k], 'j', shift(-k))  10.6 us
    pallas_call x2, Pallas kernels, products(): pl.pallas_call(functools.partial(product_kernel, mirror), out_shape=shape...  10.1 us
    ppermute x1, waiting for transfers between devices, shards(): trio = lax.ppermute(trio, ALL, turn)  7.85 us
  transfers between devices with their start and end apart: 12, of which 7 were waited for; matrix products, arithmetic and copies ran while one was open for 2% of the time, Pallas kernels for 7%

commit v1 on v0

--- a/solution.py
+++ b/solution.py
@@ -63,7 +63,7 @@
         own, tiles, keep, give, x, acc, held, sems = refs
         parts = [own]
     else:
-        mine, theirs, tiles, payload, x, acc, held, sems = refs
+        mine, theirs, tiles, acc, x, held, sems = refs
         parts = [mine, theirs]
     slots, width = tiles.shape[0], tiles.shape[1]
     chunks = slots // CHUNK
@@ -112,13 +112,6 @@
         half = keep.shape[0]
         keep[...] = acc[:half]
         give[...] = acc[half:]
-    else:
-
-        def pack_body(p, carry):
-            pack(acc[p, 0], acc[p, 1], payload, p)
-            return carry
-
-        lax.fori_loop(0, payload.shape[0], pack_body, 0, unroll=4)
 
 
 def products(mirror, meta, sources, targets, segment, tiles):
@@ -126,23 +119,25 @@
     pieces = segment[0].shape[0] * len(segment)
     vecs = segment[0].shape[1]
     slots, width = tiles.shape[:2]
+    scratch = [
+        pltpu.VMEM((pieces + 1, 2, vecs, width), jnp.bfloat16),
+        pltpu.VMEM((pieces, 2, vecs, width), jnp.float32),
+        pltpu.VMEM((slots, width, width), jnp.bfloat16),
+        pltpu.SemaphoreType.DMA((slots // CHUNK,)),
+    ]
     if mirror:
         shapes = [jax.ShapeDtypeStruct((pieces // 2, 2, vecs, width), jnp.float32)] * 2
         outs = [vmem(), vmem()]
     else:
-        shapes = jax.ShapeDtypeStruct((pieces, 5 * vecs // 2, width), jnp.int16)
+        shapes = jax.ShapeDtypeStruct((pieces, 2, vecs, width), jnp.float32)
         outs = vmem()
+        del scratch[1]
     return pl.pallas_call(
         functools.partial(product_kernel, mirror),
         out_shape=shapes,
         in_specs=[smem] * 3 + [vmem()] * len(segment) + [pl.BlockSpec(memory_space=pl.ANY)],
         out_specs=outs,
-        scratch_shapes=[
-            pltpu.VMEM((pieces + 1, 2, vecs, width), jnp.bfloat16),
-            pltpu.VMEM((pieces, 2, vecs, width), jnp.float32),
-            pltpu.VMEM((slots, width, width), jnp.bfloat16),
-            pltpu.SemaphoreType.DMA((slots // CHUNK,)),
-        ],
+        scratch_shapes=scratch,
     )(meta, sources, targets, *segment, tiles)
 
 
@@ -164,8 +159,37 @@
     )(keep, came)
 
 
-def total_kernel(kinds, vecs, payload, *refs):
-    *added, out = refs
+def merge_kernel(place, sums, trio, payload):
+    pieces, _, _, width = sums.shape
+    fold = trio.shape[0]
+    step = pieces // fold
+
+    def body(p, carry):
+        pack(sums[p, 0], sums[p, 1], payload, p)
+        return carry
+
+    lax.fori_loop(0, pieces, body, 0, unroll=4)
+    for i in range(fold):
+        p = i * step + place[0]
+        pack(
+            sums[p, 0] + trio[i, :, :width],
+            sums[p, 1] + trio[i, :, width:],
+            payload,
+            p,
+        )
+
+
+def merge(place, sums, trio):
+    pieces, _, vecs, width = sums.shape
+    return pl.pallas_call(
+        merge_kernel,
+        out_shape=jax.ShapeDtypeStruct((pieces, 5 * vecs // 2, width), jnp.int16),
+        in_specs=[pl.BlockSpec(memory_space=pltpu.SMEM)] + [vmem()] * 2,
+        out_specs=vmem(),
+    )(place, sums, trio)
+
+
+def total_kernel(kinds, vecs, payload, out):
     width = payload.shape[-1]
 
     for kind in range(kinds):
@@ -177,21 +201,17 @@
         zero = jnp.zeros((vecs, width), jnp.float32)
         sums = lax.fori_loop(0, payload.shape[0] // kinds, body, (zero, zero), unroll=4)
         for s in range(2):
-            lanes = slice(s * width, (s + 1) * width)
-            total = sums[s]
-            for other in added:
-                total = total + other[:, lanes]
-            out[kind, :, lanes] = total
-
-
-def total(kinds, vecs, payload, *added):
+            out[kind, :, s * width : (s + 1) * width] = sums[s]
+
+
+def total(kinds, vecs, payload):
     width = payload.shape[-1]
     return pl.pallas_call(
         functools.partial(total_kernel, kinds, vecs),
         out_shape=jax.ShapeDtypeStruct((kinds, vecs, 2 * width), jnp.float32),
-        in_specs=[vmem()] * (1 + len(added)),
+        in_specs=[vmem()],
         out_specs=vmem(),
-    )(payload, *added)
+    )(payload)
 
 
 def spread(array, axes):
@@ -206,10 +226,9 @@
     vecs = vectors.shape[0]
     slots = tiles.shape[0]
     row_index = lax.axis_index(("rr", "core"))
-    core, j = lax.axis_index("core"), lax.axis_index("j")
+    core = lax.axis_index("core")
     mirror_index = lax.axis_index("m")
     swap = [(0, 1), (1, 0)]
-    shift = lambda k: [(i, (i + k) % fold) for i in range(fold)]
     turn = [
         ((r * fold + i) * n_row + a, (a * fold + i) * n_row + r)
         for r in range(n_row)
@@ -219,9 +238,8 @@
 
     shard, half = tile_cols // 2, tile_cols % 2
     member = shard % n_row
-    behind = (j - shard // n_row) % fold
     place = ((member % 2) ^ core) * (n_row // 2) + member // 2
-    col_place = (place * fold + behind) * 2 + half
+    col_place = (place * fold + shard // n_row) * 2 + half
     nothing = 2 * n_row * fold
     live = jnp.arange(slots, dtype=jnp.int32) < tile_count[0]
     mirrored = live & ((row_index != mirror_index) | (tile_rows != tile_cols))
@@ -229,21 +247,22 @@
     plain_source = jnp.where(live, col_place, nothing)
 
     own = spread(vectors, ("j", "m"))
-    trio = jnp.stack([vectors] + [lax.ppermute(vectors, "j", shift(k)) for k in range(1, fold)])
+    trio = own.reshape(fold, n_row, *vectors.shape)
+    trio = lax.dynamic_index_in_dim(trio, mirror_index, 1, keepdims=False)
     trio = lax.ppermute(trio, ALL, turn)
-    own, trio = lax.optimization_barrier((own, trio))
+    keep, give = products(True, tile_count, mirror_source, col_place, [own], tiles)
+    came = lax.ppermute(give, "core", swap)
+    sums = join(keep, came)
+    sums = lax.all_to_all(sums, "rr", 0, 0, tiled=True)
+    sums = total(fold, vecs, sums)
+    sums = lax.ppermute(sums, ALL, turn)
+
     mine = spread(trio, "rr").reshape(-1, *vectors.shape)
     theirs = lax.ppermute(mine, "core", swap)
-
-    keep, give = products(True, tile_count, mirror_source, col_place, [own], tiles)
-    sums = join(keep, lax.ppermute(give, "core", swap))
-    sums = lax.all_to_all(sums, "rr", 0, 0, tiled=True)
-    sums = lax.ppermute(total(fold, vecs, sums), ALL, turn)
-    mirror_sums = [sums[0]] + [lax.ppermute(sums[k], "j", shift(-k)) for k in range(1, fold)]
-
     plain = products(False, tile_count, plain_source, tile_rows, [mine, theirs], tiles)
+    plain = merge(mirror_index[None].astype(jnp.int32), plain, sums)
     plain = lax.all_to_all(plain, ("j", "m"), 0, 0, tiled=True)
-    return total(1, vecs, plain, *mirror_sums)[0]
+    return total(1, vecs, plain)[0]
 
 
 def solution(mesh):

time: 158 us -> 157 us (level)
  the two profiles are of different devices: /device:TPU:138 before, /device:TPU:56 now
where the time goes in v1:
time: 157 us; the launch traced here: 156 us
  starting transfers between devices  54.4 us (35%)
  waiting for transfers between devices  35.5 us (23%)
  blocking collectives  35.4 us (23%)
  Pallas kernels  22.3 us (14%)
  local copies, waits for them, and re-layouts  6.4 us (4%)
    all_to_all x1, blocking collectives, shards(): plain = lax.all_to_all(plain, ('j', 'm'), 0, 0, tiled=True)  35.4 us
    all_to_all x2, starting transfers between devices, spread(): lax.all_to_all(jnp.broadcast_to(array[None], (size, *array.shape)), axes,...  32.6 us
    all_to_all x2, waiting for transfers between devices, spread(): lax.all_to_all(jnp.broadcast_to(array[None], (size, *array.shape)), axes,...  21.1 us
    pallas_call x2, Pallas kernels, products(): pl.pallas_call(functools.partial(product_kernel, mirror), out_shape=shape...  11.3 us
    all_to_all x1, starting transfers between devices, shards(): sums = lax.all_to_all(sums, 'rr', 0, 0, tiled=True)  8.41 us
    ppermute x1, waiting for transfers between devices, shards(): trio = lax.ppermute(trio, ALL, turn)  8.12 us
    ppermute x1, starting transfers between devices, shards(): sums = lax.ppermute(sums, ALL, turn)  4.98 us
    pallas_call x2, Pallas kernels, total(): pl.pallas_call(functools.partial(total_kernel, kinds, vecs), out_shape=ja...  4.96 us
  transfers between devices with their start and end apart: 7, of which 5 were waited for; matrix products, arithmetic and copies ran while one was open for 2% of the time, Pallas kernels for 7%

profile of v1, /device:TPU:56, one launch (start us, length us, event | category | flops | bytes accessed | tf_op | source)
XLA Modules:
  0.0 156.0 jit_solution(9209582333017305171)
XLA Ops:
  0.0 1.5 broadcast_in_dim.22
  1.5 18.9 %all-to-all-start = ((bf16[48,16,256]{2,1,0:T(8,128)(2,1)}), bf16[48,16,256]{2,1,0:T(8,128)(2,1)S(1)}, u32[]{:S(2)}, u32[]{:S(2)}) async-start(bf16[48,16,256]{2,1,0:T(8,128)(2,1)} %broadcast_in_dim.22), calls=%async_computation | async-start | bytes 786432 | tf_op jit(solution)/shard_map/all_to_all | solution.py:219
  21.0 1.3 compare_select_fusion.9
  22.3 18.6 %all-to-all-done.refs_0_ = bf16[48,16,256]{2,1,0:T(8,128)(2,1)S(1)} async-done(((bf16[48,16,256]{2,1,0:T(8,128)(2,1)}), bf16[48,16,256]{2,1,0:T(8,128)(2,1)S(1)}, u32[]{:S(2)}, u32[]{:S(2)}) %all-to-all-start) | async-done | bytes 393248 | tf_op jit(solution)/shard_map/all_to_all | solution.py:219
  40.9 0.0 copy-start
  40.9 0.8 copy-done
  41.7 5.1 %shard_map.56 = (f32[24,2,16,128]{3,2,1,0:T(8,128)}, f32[24,2,16,128]{3,2,1,0:T(8,128)}) custom-call(s32[1]{0:T(128)} %copy.6.meta, s32[128]{0:T(128)} %get-tuple-element.11.sources, s32[128]{0:T(128)} %get-tuple-element.10.targets, bf16[48,16,256]{2,1,0:T(8,128)(2,1)} %copy-done, bf16[128,128,128]{2,1,0:T(8,128)(2,1)} %refs_1_.1), custom_call_target="tpu_custom_call" | custom-call | tf_op jit(solution)/shard_map/pallas_call | solution.py:135
  46.8 1.9 %collective-permute-start.2 = (f32[24,2,16,128]{3,2,1,0:T(8,128)}, f32[24,2,16,128]{3,2,1,0:T(8,128)S(1)}, u32[]{:S(2)}, u32[]{:S(2)}) collective-permute-start(f32[24,2,16,128]{3,2,1,0:T(8,128)} %get-tuple-element.8), channel_id=1, source_target_pairs={{0,48},{48,0},{1,49},{49,1},{2,50},{50,2},{3,51},{51,3},{4,52},{52... | collective-permute-start | bytes 1179656 | tf_op jit(solution)/shard_map/ppermute | solution.py:254
  48.8 0.8 dynamic-slice_bitcast_fusion
  49.5 4.6 %collective-permute-start = (bf16[3,16,256]{2,1,0:T(8,128)(2,1)S(1)}, bf16[3,16,256]{2,1,0:T(8,128)(2,1)S(1)}, u32[]{:S(2)}, u32[]{:S(2)}) collective-permute-start(bf16[3,16,256]{2,1,0:T(8,128)(2,1)S(1)} %dynamic-slice_bitcast_fusion), channel_id=1, source_target_pairs={{0,0},{1,48},{2,96},{3,144},{4,192},{5,240},{6,288},{7,336},{8,384... | collective-permute-start | bytes 73736 | tf_op jit(solution)/shard_map/ppermute | solution.py:252
  54.2 8.1 %collective-permute-done = bf16[3,16,256]{2,1,0:T(8,128)(2,1)S(1)} collective-permute-done((bf16[3,16,256]{2,1,0:T(8,128)(2,1)S(1)}, bf16[3,16,256]{2,1,0:T(8,128)(2,1)S(1)}, u32[]{:S(2)}, u32[]{:S(2)}) %collective-permute-start) | collective-permute-done | bytes 24608 | tf_op jit(solution)/shard_map/ppermute | solution.py:252
  62.3 0.7 broadcast_in_dim.23
  63.0 13.7 %all-to-all-start.1 = ((bf16[8,3,16,256]{3,2,1,0:T(8,128)(2,1)}), bf16[8,3,16,256]{3,2,1,0:T(8,128)(2,1)S(1)}, u32[]{:S(2)}, u32[]{:S(2)}) async-start(bf16[8,3,16,256]{3,2,1,0:T(8,128)(2,1)} %broadcast_in_dim.23), calls=%async_computation.1 | async-start | bytes 393216 | tf_op jit(solution)/shard_map/all_to_all | solution.py:219
  76.7 0.0 collective-permute-done.2.came
  76.7 0.0 copy-start.3
  76.7 0.7 copy-done.3
  77.4 2.5 %shard_map.57 = s16[24,40,128]{2,1,0:T(8,128)(2,1)} custom-call(f32[24,2,16,128]{3,2,1,0:T(8,128)} %get-tuple-element.7.keep, f32[24,2,16,128]{3,2,1,0:T(8,128)} %copy-done.3), custom_call_target="tpu_custom_call" | custom-call | tf_op jit(solution)/shard_map/pallas_call | solution.py:154
  80.0 2.5 %all-to-all-done.1 = bf16[8,3,16,256]{3,2,1,0:T(8,128)(2,1)S(1)} async-done(((bf16[8,3,16,256]{3,2,1,0:T(8,128)(2,1)}), bf16[8,3,16,256]{3,2,1,0:T(8,128)(2,1)S(1)}, u32[]{:S(2)}, u32[]{:S(2)}) %all-to-all-start.1) | async-done | bytes 196640 | tf_op jit(solution)/shard_map/all_to_all | solution.py:219
  82.5 0.0 copy-start.2
  82.5 8.4 %all-to-all-start.2 = ((s16[24,40,128]{2,1,0:T(8,128)(2,1)}), s16[24,40,128]{2,1,0:T(8,128)(2,1)S(1)}, u32[]{:S(2)}, u32[]{:S(2)}) async-start(s16[24,40,128]{2,1,0:T(8,128)(2,1)} %shard_map.57), calls=%async_computation.2 | async-start | bytes 491520 | tf_op jit(solution)/shard_map/all_to_all | solution.py:256
  90.9 1.9 %collective-permute-start.1 = (bf16[24,16,256]{2,1,0:T(8,128)(2,1)S(1)}, bf16[24,16,256]{2,1,0:T(8,128)(2,1)S(1)}, u32[]{:S(2)}, u32[]{:S(2)}) collective-permute-start(bf16[24,16,256]{2,1,0:T(8,128)(2,1)S(1)} %bitcast.9), channel_id=1, source_target_pairs={{0,48},{48,0},{1,49},{49,1},{2,50},{50,2},{3,51},{51,3},{4,52},{52... | collective-permute-start | bytes 589832 | tf_op jit(solution)/shard_map/ppermute | solution.py:261
  92.8 4.9 %all-to-all-done.2.payload = s16[24,40,128]{2,1,0:T(8,128)(2,1)S(1)} async-done(((s16[24,40,128]{2,1,0:T(8,128)(2,1)}), s16[24,40,128]{2,1,0:T(8,128)(2,1)S(1)}, u32[]{:S(2)}, u32[]{:S(2)}) %all-to-all-start.2) | async-done | bytes 245792 | tf_op jit(solution)/shard_map/all_to_all | solution.py:256
  97.7 0.0 copy-start.1
  97.7 0.7 copy-done.1
  98.4 2.2 %shard_map.58 = f32[3,16,256]{2,1,0:T(8,128)} custom-call(s16[24,40,128]{2,1,0:T(8,128)(2,1)} %copy-done.1), custom_call_target="tpu_custom_call" | custom-call | tf_op jit(solution)/shard_map/pallas_call | solution.py:209
  100.5 5.0 %collective-permute-start.3 = (f32[3,16,256]{2,1,0:T(8,128)}, f32[3,16,256]{2,1,0:T(8,128)S(1)}, u32[]{:S(2)}, u32[]{:S(2)}) collective-permute-start(f32[3,16,256]{2,1,0:T(8,128)} %shard_map.58), channel_id=1, source_target_pairs={{0,0},{1,48},{2,96},{3,144},{4,192},{5,240},{6,288},{7,336},{8,384... | collective-permute-start | bytes 147464 | tf_op jit(solution)/shard_map/ppermute | solution.py:258
  105.5 0.0 collective-permute-done.1.refs_1_
  105.5 0.0 copy-start.4
  105.5 0.0 copy-done.2
  105.5 0.7 copy-done.4
  106.2 6.2 %shard_map.55.sums = f32[48,2,16,128]{3,2,1,0:T(8,128)} custom-call(s32[1]{0:T(128)} %copy.6.meta, s32[128]{0:T(128)} %get-tuple-element.9.sources, s32[128]{0:T(128)} %targets.1, bf16[24,16,256]{2,1,0:T(8,128)(2,1)} %bitcast.10, bf16[24,16,256]{2,1,0:T(8,128)(2,1)} %copy-done.4, bf16[128,128,128]{2,1,0:T(8,128)(2,1)} %refs_1_.1), custom_call_target="tpu_custom_call" | custom-call | tf_op jit(solution)/shard_map/pallas_call | solution.py:135
  112.4 1.4 collective-permute-done.3.trio
  113.8 0.0 copy-start.5
  113.8 0.6 copy-done.5
  114.4 3.5 %shard_map.59 = s16[48,40,128]{2,1,0:T(8,128)(2,1)} custom-call(s32[1]{0:T(128)} %bitcast.place, f32[48,2,16,128]{3,2,1,0:T(8,128)} %shard_map.55.sums, f32[3,16,256]{2,1,0:T(8,128)} %copy-done.5), custom_call_target="tpu_custom_call" | custom-call | tf_op jit(solution)/shard_map/pallas_call | solution.py:184
  117.9 35.4 %all_to_all.20.payload = s16[48,40,128]{2,1,0:T(8,128)(2,1)} all-to-all(s16[48,40,128]{2,1,0:T(8,128)(2,1)} %shard_map.59), channel_id=1, replica_groups=mesh['rr'=8,'core'=2,'j'=3,'m'=16] {'j','m'}, dimensions={0} | all-to-all | bytes 983040 | tf_op jit(solution)/shard_map/all_to_all | solution.py:264
  153.2 2.8 %shard_map.60 = f32[1,16,256]{2,1,0:T(8,128)} custom-call(s16[48,40,128]{2,1,0:T(8,128)(2,1)} %all_to_all.20.payload), custom_call_target="tpu_custom_call" | custom-call | tf_op jit(solution)/shard_map/pallas_call | solution.py:209
Async XLA Ops:
  1.5 39.5 %all-to-all-start = ((bf16[48,16,256]{2,1,0:T(8,128)(2,1)}), bf16[48,16,256]{2,1,0:T(8,128)(2,1)S(1)}, u32[]{:S(2)}, u32[]{:S(2)}) async-start(bf16[48,16,256]{2,1,0:T(8,128)(2,1)} %broadcast_in_dim.22), calls=%async_computation | async-start | bytes 786432 | tf_op jit(solution)/shard_map/all_to_all | solution.py:219
  40.9 0.8 copy-start
  46.8 29.9 %collective-permute-start.2 = (f32[24,2,16,128]{3,2,1,0:T(8,128)}, f32[24,2,16,128]{3,2,1,0:T(8,128)S(1)}, u32[]{:S(2)}, u32[]{:S(2)}) collective-permute-start(f32[24,2,16,128]{3,2,1,0:T(8,128)} %get-tuple-element.8), channel_id=1, source_target_pairs={{0,48},{48,0},{1,49},{49,1},{2,50},{50,2},{3,51},{51,3},{4,52},{52... | collective-permute-start | bytes 1179656 | tf_op jit(solution)/shard_map/ppermute | solution.py:254
  49.5 12.8 %collective-permute-start = (bf16[3,16,256]{2,1,0:T(8,128)(2,1)S(1)}, bf16[3,16,256]{2,1,0:T(8,128)(2,1)S(1)}, u32[]{:S(2)}, u32[]{:S(2)}) collective-permute-start(bf16[3,16,256]{2,1,0:T(8,128)(2,1)S(1)} %dynamic-slice_bitcast_fusion), channel_id=1, source_target_pairs={{0,0},{1,48},{2,96},{3,144},{4,192},{5,240},{6,288},{7,336},{8,384... | collective-permute-start | bytes 73736 | tf_op jit(solution)/shard_map/ppermute | solution.py:252
  63.0 19.5 %all-to-all-start.1 = ((bf16[8,3,16,256]{3,2,1,0:T(8,128)(2,1)}), bf16[8,3,16,256]{3,2,1,0:T(8,128)(2,1)S(1)}, u32[]{:S(2)}, u32[]{:S(2)}) async-start(bf16[8,3,16,256]{3,2,1,0:T(8,128)(2,1)} %broadcast_in_dim.23), calls=%async_computation.1 | async-start | bytes 393216 | tf_op jit(solution)/shard_map/all_to_all | solution.py:219
  76.7 0.7 copy-start.3
  82.5 23.1 %copy-start.2 = (bf16[8,3,16,256]{3,2,1,0:T(8,128)(2,1)}, bf16[8,3,16,256]{3,2,1,0:T(8,128)(2,1)S(1)}, u32[]{:S(2)}) copy-start(bf16[8,3,16,256]{3,2,1,0:T(8,128)(2,1)S(1)} %all-to-all-done.1) | copy-start | bytes 589828
  82.5 15.2 %all-to-all-start.2 = ((s16[24,40,128]{2,1,0:T(8,128)(2,1)}), s16[24,40,128]{2,1,0:T(8,128)(2,1)S(1)}, u32[]{:S(2)}, u32[]{:S(2)}) async-start(s16[24,40,128]{2,1,0:T(8,128)(2,1)} %shard_map.57), calls=%async_computation.2 | async-start | bytes 491520 | tf_op jit(solution)/shard_map/all_to_all | solution.py:256
  90.9 14.6 %collective-permute-start.1 = (bf16[24,16,256]{2,1,0:T(8,128)(2,1)S(1)}, bf16[24,16,256]{2,1,0:T(8,128)(2,1)S(1)}, u32[]{:S(2)}, u32[]{:S(2)}) collective-permute-start(bf16[24,16,256]{2,1,0:T(8,128)(2,1)S(1)} %bitcast.9), channel_id=1, source_target_pairs={{0,48},{48,0},{1,49},{49,1},{2,50},{50,2},{3,51},{51,3},{4,52},{52... | collective-permute-start | bytes 589832 | tf_op jit(solution)/shard_map/ppermute | solution.py:261
  97.7 0.7 copy-start.1
  100.5 13.3 %collective-permute-start.3 = (f32[3,16,256]{2,1,0:T(8,128)}, f32[3,16,256]{2,1,0:T(8,128)S(1)}, u32[]{:S(2)}, u32[]{:S(2)}) collective-permute-start(f32[3,16,256]{2,1,0:T(8,128)} %shard_map.58), channel_id=1, source_target_pairs={{0,0},{1,48},{2,96},{3,144},{4,192},{5,240},{6,288},{7,336},{8,384... | collective-permute-start | bytes 147464 | tf_op jit(solution)/shard_map/ppermute | solution.py:258
  105.5 0.7 copy-start.4
  113.8 0.6 copy-start.5

commit v2 on v1

--- a/solution.py
+++ b/solution.py
@@ -5,11 +5,10 @@
 from jax import lax
 from jax.experimental import pallas as pl
 from jax.experimental.pallas import tpu as pltpu
-from jax.sharding import Mesh, PartitionSpec as P
+from jax.sharding import PartitionSpec as P
 
 CHUNK = 16
 TOP = 14
-ALL = ("rr", "core", "j", "m")
 
 
 def vmem():
@@ -159,59 +158,110 @@
     )(keep, came)
 
 
-def merge_kernel(place, sums, trio, payload):
-    pieces, _, _, width = sums.shape
-    fold = trio.shape[0]
-    step = pieces // fold
-
-    def body(p, carry):
-        pack(sums[p, 0], sums[p, 1], payload, p)
+def merge_kernel(side, sums, came, payload):
+    pieces, _, vecs, _ = sums.shape
+    half = pieces // 2
+    first, other = side[0] * half, (1 - side[0]) * half
+
+    def body(i, carry):
+        left, right = unpack(came, i, vecs)
+        pack(sums[first + i, 0] + left, sums[first + i, 1] + right, payload, first + i)
+        pack(sums[other + i, 0], sums[other + i, 1], payload, other + i)
         return carry
 
-    lax.fori_loop(0, pieces, body, 0, unroll=4)
-    for i in range(fold):
-        p = i * step + place[0]
-        pack(
-            sums[p, 0] + trio[i, :, :width],
-            sums[p, 1] + trio[i, :, width:],
-            payload,
-            p,
-        )
-
-
-def merge(place, sums, trio):
+    lax.fori_loop(0, half, body, 0, unroll=2)
+
+
+def merge(side, sums, came):
     pieces, _, vecs, width = sums.shape
     return pl.pallas_call(
         merge_kernel,
         out_shape=jax.ShapeDtypeStruct((pieces, 5 * vecs // 2, width), jnp.int16),
         in_specs=[pl.BlockSpec(memory_space=pltpu.SMEM)] + [vmem()] * 2,
         out_specs=vmem(),
-    )(place, sums, trio)
-
-
-def total_kernel(kinds, vecs, payload, out):
+    )(side, sums, came)
+
+
+def total_kernel(vecs, payload, out):
     width = payload.shape[-1]
 
-    for kind in range(kinds):
-
-        def body(i, sums, kind=kind):
-            left, right = unpack(payload, i * kinds + kind, vecs)
-            return sums[0] + left, sums[1] + right
-
-        zero = jnp.zeros((vecs, width), jnp.float32)
-        sums = lax.fori_loop(0, payload.shape[0] // kinds, body, (zero, zero), unroll=4)
-        for s in range(2):
-            out[kind, :, s * width : (s + 1) * width] = sums[s]
-
-
-def total(kinds, vecs, payload):
-    width = payload.shape[-1]
+    def body(i, sums):
+        left, right = unpack(payload, i, vecs)
+        return sums[0] + left, sums[1] + right
+
+    zero = jnp.zeros((vecs, width), jnp.float32)
+    sums = lax.fori_loop(0, payload.shape[0], body, (zero, zero), unroll=4)
+    for s in range(2):
+        out[:, s * width : (s + 1) * width] = sums[s]
+
+
+def total(vecs, payload):
     return pl.pallas_call(
-        functools.partial(total_kernel, kinds, vecs),
-        out_shape=jax.ShapeDtypeStruct((kinds, vecs, 2 * width), jnp.float32),
+        functools.partial(total_kernel, vecs),
+        out_shape=jax.ShapeDtypeStruct((vecs, 2 * payload.shape[-1]), jnp.float32),
         in_specs=[vmem()],
         out_specs=vmem(),
     )(payload)
+
+
+def assign(cost):
+    n = len(cost)
+    row_price, col_price = [0] * (n + 1), [0] * (n + 1)
+    owner, trail = [0] * (n + 1), [0] * (n + 1)
+    for i in range(1, n + 1):
+        owner[0], at = i, 0
+        slack, seen = [float("inf")] * (n + 1), [False] * (n + 1)
+        while owner[at]:
+            seen[at] = True
+            row, gap, nearest = owner[at], float("inf"), 0
+            for c in range(1, n + 1):
+                if not seen[c]:
+                    left = cost[row - 1][c - 1] - row_price[row] - col_price[c]
+                    if left < slack[c]:
+                        slack[c], trail[c] = left, at
+                    if slack[c] < gap:
+                        gap, nearest = slack[c], c
+            for c in range(n + 1):
+                if seen[c]:
+                    row_price[owner[c]] += gap
+                    col_price[c] -= gap
+                else:
+                    slack[c] -= gap
+            at = nearest
+        while at:
+            owner[at] = owner[trail[at]]
+            at = trail[at]
+    columns = [0] * n
+    for c in range(1, n + 1):
+        columns[owner[c] - 1] = c - 1
+    return columns
+
+
+def position(row, col, n_col):
+    deep = n_col // 4
+    return row // 4, (row // 2) % 2 * 4 + col // deep, col % deep
+
+
+def hops(one, other, sides=(4, 8, 12)):
+    return [min((p - q) % side, (q - p) % side) for p, q, side in zip(one, other, sides)]
+
+
+def handing(n_row, n_col):
+    pairs = []
+    for m in range(n_row):
+        takers = [(r, c) for c in range(m, n_col, n_row) for r in range(n_row)]
+        cost = []
+        for c in range(n_col):
+            start = position(m, c, n_col)
+            line = []
+            for r, col in takers:
+                far = sum(h * h + 4 * h for h in hops(start, position(r, col, n_col)))
+                line.append(far + (100000 if r % 2 != c % 2 else 0))
+            cost.append(line)
+        for c, taker in enumerate(assign(cost)):
+            r, col = takers[taker]
+            pairs.append((m * n_col + c, r * n_col + col))
+    return pairs
 
 
 def spread(array, axes):
@@ -221,58 +271,48 @@
     )
 
 
-def shards(vectors, tiles, tile_rows, tile_cols, tile_count):
-    n_row, fold = lax.axis_size("m"), lax.axis_size("j")
-    vecs = vectors.shape[0]
-    slots = tiles.shape[0]
-    row_index = lax.axis_index(("rr", "core"))
-    core = lax.axis_index("core")
-    mirror_index = lax.axis_index("m")
-    swap = [(0, 1), (1, 0)]
-    turn = [
-        ((r * fold + i) * n_row + a, (a * fold + i) * n_row + r)
-        for r in range(n_row)
-        for i in range(fold)
-        for a in range(n_row)
-    ]
-
-    shard, half = tile_cols // 2, tile_cols % 2
-    member = shard % n_row
-    place = ((member % 2) ^ core) * (n_row // 2) + member // 2
-    col_place = (place * fold + shard // n_row) * 2 + half
-    nothing = 2 * n_row * fold
+def shards(pairs, vectors, tiles, tile_rows, tile_cols, tile_count):
+    axes = ("row", "col")
+    n_row, n_col = lax.axis_size("row"), lax.axis_size("col")
+    vecs, slots = vectors.shape[0], tiles.shape[0]
+    pieces = n_col // 2
+    row_index, col_index = lax.axis_index("row"), lax.axis_index("col")
+    core, side = row_index % 2, col_index % 2
+    swap = [(r, r ^ 1) for r in range(n_row)]
+
+    col_place = ((tile_cols // n_col) ^ core) * n_col + tile_cols % n_col
+    nothing = 2 * n_col
     live = jnp.arange(slots, dtype=jnp.int32) < tile_count[0]
-    mirrored = live & ((row_index != mirror_index) | (tile_rows != tile_cols))
+    mirrored = live & ((row_index != col_index % n_row) | (tile_rows != tile_cols))
     mirror_source = jnp.where(mirrored, tile_rows, nothing)
     plain_source = jnp.where(live, col_place, nothing)
 
-    own = spread(vectors, ("j", "m"))
-    trio = own.reshape(fold, n_row, *vectors.shape)
-    trio = lax.dynamic_index_in_dim(trio, mirror_index, 1, keepdims=False)
-    trio = lax.ppermute(trio, ALL, turn)
+    own = spread(vectors, "col")
+    mine = lax.dynamic_slice_in_dim(own, side * pieces, pieces, 0)
+    mine = lax.ppermute(mine, axes, pairs)
     keep, give = products(True, tile_count, mirror_source, col_place, [own], tiles)
-    came = lax.ppermute(give, "core", swap)
+    came = lax.ppermute(give, "row", swap)
     sums = join(keep, came)
-    sums = lax.all_to_all(sums, "rr", 0, 0, tiled=True)
-    sums = total(fold, vecs, sums)
-    sums = lax.ppermute(sums, ALL, turn)
-
-    mine = spread(trio, "rr").reshape(-1, *vectors.shape)
-    theirs = lax.ppermute(mine, "core", swap)
+    sums = lax.ppermute(sums, axes, [(taker, giver) for giver, taker in pairs])
+
+    theirs = lax.ppermute(mine, "row", swap)
     plain = products(False, tile_count, plain_source, tile_rows, [mine, theirs], tiles)
-    plain = merge(mirror_index[None].astype(jnp.int32), plain, sums)
-    plain = lax.all_to_all(plain, ("j", "m"), 0, 0, tiled=True)
-    return total(1, vecs, plain)[0]
+    plain = merge(side[None].astype(jnp.int32), plain, sums)
+    plain = lax.all_to_all(plain, "col", 0, 0, tiled=True)
+    return total(vecs, plain)
 
 
 def solution(mesh):
-    n_row, n_col = mesh.shape["row"], mesh.shape["col"]
-    fine = Mesh(mesh.devices.reshape(n_row // 2, 2, n_col // n_row, n_row), ALL)
-
+    pairs = handing(mesh.shape["row"], mesh.shape["col"])
+
+    def step(*args):
+        return shards(pairs, *args)
+
+    both = ("row", "col")
     return jax.shard_map(
-        shards,
-        mesh=fine,
-        in_specs=(P(None, ALL), P(ALL, None, None), P(ALL), P(ALL), P(ALL)),
-        out_specs=P(None, ALL),
+        step,
+        mesh=mesh,
+        in_specs=(P(None, both), P(both, None, None), P(both), P(both), P(both)),
+        out_specs=P(None, both),
         check_vma=False,
     )

time: 157 us -> 131 us (0.83)
  the two profiles are of different devices: /device:TPU:56 before, /device:TPU:6 now
where the time goes in v2:
time: 131 us
  blocking collectives  49 us (37%)
  starting transfers between devices  33.7 us (26%)
  waiting for transfers between devices  21 us (16%)
  Pallas kernels  19.6 us (15%)
  local copies, waits for them, and re-layouts  5.25 us (4%)
    all_to_all x1, blocking collectives, shards(): plain = lax.all_to_all(plain, 'col', 0, 0, tiled=True)  49 us
    all_to_all x1, waiting for transfers between devices, spread(): lax.all_to_all(jnp.broadcast_to(array[None], (size, *array.shape)), axes,...  19.6 us
    all_to_all x1, starting transfers between devices, spread(): lax.all_to_all(jnp.broadcast_to(array[None], (size, *array.shape)), axes,...  18.9 us
    pallas_call x2, Pallas kernels, products(): pl.pallas_call(functools.partial(product_kernel, mirror), out_shape=shape...  10 us
    ppermute x1, starting transfers between devices, shards(): sums = lax.ppermute(sums, axes, [(taker, giver) for giver, taker in pairs])  8.14 us
    pallas_call x1, Pallas kernels, merge(): pl.pallas_call(merge_kernel, out_shape=jax.ShapeDtypeStruct((pieces, 5 *...  4.31 us
    unnamed x10, local copies, waits for them, and re-layouts  2.85 us
    ppermute x1, starting transfers between devices, shards(): mine = lax.ppermute(mine, axes, pairs)  2.81 us
  transfers between devices with their start and end apart: 5, of which 2 were waited for; matrix products, arithmetic and copies ran while one was open for 2% of the time, Pallas kernels for 6%

profile of v2, /device:TPU:6, one launch (start us, length us, event | category | flops | bytes accessed | tf_op | source)
XLA Modules:
  0.0 130.7 jit_solution(4321275965519248415)
XLA Ops:
  0.0 1.5 %broadcast_in_dim.16 = bf16[48,16,256]{2,1,0:T(8,128)(2,1)} broadcast(bf16[16,256]{1,0:T(8,128)(2,1)} %param.5), dimensions={1,2} | broadcast | bytes 401408 | tf_op jit(solution)/shard_map/broadcast_in_dim | solution.py:270
  1.5 18.9 %all-to-all-start = ((bf16[48,16,256]{2,1,0:T(8,128)(2,1)}), bf16[48,16,256]{2,1,0:T(8,128)(2,1)S(1)}, u32[]{:S(2)}, u32[]{:S(2)}) async-start(bf16[48,16,256]{2,1,0:T(8,128)(2,1)} %broadcast_in_dim.16), calls=%async_computation | async-start | bytes 786432 | tf_op jit(solution)/shard_map/all_to_all | solution.py:269
  21.0 1.3 compare_select_fusion
  22.3 19.6 %all-to-all-done.refs_0_ = bf16[48,16,256]{2,1,0:T(8,128)(2,1)S(1)} async-done(((bf16[48,16,256]{2,1,0:T(8,128)(2,1)}), bf16[48,16,256]{2,1,0:T(8,128)(2,1)S(1)}, u32[]{:S(2)}, u32[]{:S(2)}) %all-to-all-start) | async-done | bytes 393248 | tf_op jit(solution)/shard_map/all_to_all | solution.py:269
  41.9 0.0 copy-start
  41.9 0.7 copy-done
  42.7 4.6 %shard_map.56 = (f32[24,2,16,128]{3,2,1,0:T(8,128)}, f32[24,2,16,128]{3,2,1,0:T(8,128)}) custom-call(s32[1]{0:T(128)} %copy.6.meta, s32[128]{0:T(128)} %get-tuple-element.11.sources, s32[128]{0:T(128)} %get-tuple-element.10.targets, bf16[48,16,256]{2,1,0:T(8,128)(2,1)} %copy-done, bf16[128,128,128]{2,1,0:T(8,128)(2,1)} %refs_1_.1), custom_call_target="tpu_custom_call" | custom-call | tf_op jit(solution)/shard_map/pallas_call | solution.py:134
  47.3 1.9 %collective-permute-start.2 = (f32[24,2,16,128]{3,2,1,0:T(8,128)}, f32[24,2,16,128]{3,2,1,0:T(8,128)S(1)}, u32[]{:S(2)}, u32[]{:S(2)}) collective-permute-start(f32[24,2,16,128]{3,2,1,0:T(8,128)} %get-tuple-element.8), channel_id=1, source_target_pairs={{0,48},{48,0},{96,144},{144,96},{192,240},{240,192},{288,336},{336... | collective-permute-start | bytes 1179656 | tf_op jit(solution)/shard_map/ppermute | solution.py:294
  49.3 0.9 constant_dynamic-slice_fusion
  50.2 2.8 %collective-permute-start = (bf16[24,16,256]{2,1,0:T(8,128)(2,1)S(1)}, bf16[24,16,256]{2,1,0:T(8,128)(2,1)S(1)}, u32[]{:S(2)}, u32[]{:S(2)}) collective-permute-start(bf16[24,16,256]{2,1,0:T(8,128)(2,1)S(1)} %constant_dynamic-slice_fusion), channel_id=1, source_target_pairs={{0,0},{1,48},{2,384},{3,64},{4,112},{5,256},{6,320},{7,368},{8,128... | collective-permute-start | bytes 589832 | tf_op jit(solution)/shard_map/ppermute | solution.py:292
  53.0 0.0 collective-permute-done.2.came
  53.0 0.0 copy-start.1
  53.0 0.7 copy-done.1
  53.8 2.5 %shard_map.57 = s16[24,40,128]{2,1,0:T(8,128)(2,1)} custom-call(f32[24,2,16,128]{3,2,1,0:T(8,128)} %get-tuple-element.7.keep, f32[24,2,16,128]{3,2,1,0:T(8,128)} %copy-done.1), custom_call_target="tpu_custom_call" | custom-call | tf_op jit(solution)/shard_map/pallas_call | solution.py:153
  56.3 8.1 %collective-permute-start.3 = (s16[24,40,128]{2,1,0:T(8,128)(2,1)}, s16[24,40,128]{2,1,0:T(8,128)(2,1)S(1)}, u32[]{:S(2)}, u32[]{:S(2)}) collective-permute-start(s16[24,40,128]{2,1,0:T(8,128)(2,1)} %shard_map.57), channel_id=1, source_target_pairs={{0,0},{48,1},{384,2},{64,3},{112,4},{256,5},{320,6},{368,7},{128,8... | collective-permute-start | bytes 737288 | tf_op jit(solution)/shard_map/ppermute | solution.py:296
  64.4 0.0 collective-permute-done.refs_0_
  64.5 0.0 copy-start.3
  64.5 1.9 %collective-permute-start.1 = (bf16[24,16,256]{2,1,0:T(8,128)(2,1)S(1)}, bf16[24,16,256]{2,1,0:T(8,128)(2,1)S(1)}, u32[]{:S(2)}, u32[]{:S(2)}) collective-permute-start(bf16[24,16,256]{2,1,0:T(8,128)(2,1)S(1)} %collective-permute-done.refs_0_), channel_id=1, source_target_pairs={{0,48},{48,0},{96,144},{144,96},{192,240},{240,192},{288,336},{336... | collective-permute-start | bytes 589832 | tf_op jit(solution)/shard_map/ppermute | solution.py:298
  66.4 1.4 %collective-permute-done.1.refs_1_ = bf16[24,16,256]{2,1,0:T(8,128)(2,1)S(1)} collective-permute-done((bf16[24,16,256]{2,1,0:T(8,128)(2,1)S(1)}, bf16[24,16,256]{2,1,0:T(8,128)(2,1)S(1)}, u32[]{:S(2)}, u32[]{:S(2)}) %collective-permute-start.1) | collective-permute-done | bytes 196640 | tf_op jit(solution)/shard_map/ppermute | solution.py:298
  67.8 0.0 copy-start.4
  67.8 0.0 copy-done.3
  67.8 0.7 copy-done.4
  68.5 5.4 %shard_map.55.sums = f32[48,2,16,128]{3,2,1,0:T(8,128)} custom-call(s32[1]{0:T(128)} %copy.6.meta, s32[128]{0:T(128)} %get-tuple-element.9.sources, s32[128]{0:T(128)} %targets.1, bf16[24,16,256]{2,1,0:T(8,128)(2,1)} %copy-done.3, bf16[24,16,256]{2,1,0:T(8,128)(2,1)} %copy-done.4, bf16[128,128,128]{2,1,0:T(8,128)(2,1)} %refs_1_.1), custom_call_target="tpu_custom_call" | custom-call | tf_op jit(solution)/shard_map/pallas_call | solution.py:134
  73.9 0.0 collective-permute-done.3.came
  73.9 0.0 copy-start.2
  73.9 0.7 copy-done.2
  74.6 4.3 %shard_map.58 = s16[48,40,128]{2,1,0:T(8,128)(2,1)} custom-call(s32[1]{0:T(128)} %bitcast.side, f32[48,2,16,128]{3,2,1,0:T(8,128)} %shard_map.55.sums, s16[24,40,128]{2,1,0:T(8,128)(2,1)} %copy-done.2), custom_call_target="tpu_custom_call" | custom-call | tf_op jit(solution)/shard_map/pallas_call | solution.py:177
  78.9 49.0 %all_to_all.10.payload = s16[48,40,128]{2,1,0:T(8,128)(2,1)} all-to-all(s16[48,40,128]{2,1,0:T(8,128)(2,1)} %shard_map.58), channel_id=1, replica_groups=mesh['row'=16,'col'=48] {'col'}, dimensions={0} | all-to-all | bytes 983040 | tf_op jit(solution)/shard_map/all_to_all | solution.py:301
  127.9 2.8 %shard_map.59 = f32[16,256]{1,0:T(8,128)} custom-call(s16[48,40,128]{2,1,0:T(8,128)(2,1)} %all_to_all.10.payload), custom_call_target="tpu_custom_call" | custom-call | tf_op jit(solution)/shard_map/pallas_call | solution.py:199
Async XLA Ops:
  1.5 40.5 %all-to-all-start = ((bf16[48,16,256]{2,1,0:T(8,128)(2,1)}), bf16[48,16,256]{2,1,0:T(8,128)(2,1)S(1)}, u32[]{:S(2)}, u32[]{:S(2)}) async-start(bf16[48,16,256]{2,1,0:T(8,128)(2,1)} %broadcast_in_dim.16), calls=%async_computation | async-start | bytes 786432 | tf_op jit(solution)/shard_map/all_to_all | solution.py:269
  41.9 0.7 copy-start
  47.3 5.7 %collective-permute-start.2 = (f32[24,2,16,128]{3,2,1,0:T(8,128)}, f32[24,2,16,128]{3,2,1,0:T(8,128)S(1)}, u32[]{:S(2)}, u32[]{:S(2)}) collective-permute-start(f32[24,2,16,128]{3,2,1,0:T(8,128)} %get-tuple-element.8), channel_id=1, source_target_pairs={{0,48},{48,0},{96,144},{144,96},{192,240},{240,192},{288,336},{336... | collective-permute-start | bytes 1179656 | tf_op jit(solution)/shard_map/ppermute | solution.py:294
  50.2 14.2 %collective-permute-start = (bf16[24,16,256]{2,1,0:T(8,128)(2,1)S(1)}, bf16[24,16,256]{2,1,0:T(8,128)(2,1)S(1)}, u32[]{:S(2)}, u32[]{:S(2)}) collective-permute-start(bf16[24,16,256]{2,1,0:T(8,128)(2,1)S(1)} %constant_dynamic-slice_fusion), channel_id=1, source_target_pairs={{0,0},{1,48},{2,384},{3,64},{4,112},{5,256},{6,320},{7,368},{8,128... | collective-permute-start | bytes 589832 | tf_op jit(solution)/shard_map/ppermute | solution.py:292
  53.0 0.7 copy-start.1
  56.3 17.6 %collective-permute-start.3 = (s16[24,40,128]{2,1,0:T(8,128)(2,1)}, s16[24,40,128]{2,1,0:T(8,128)(2,1)S(1)}, u32[]{:S(2)}, u32[]{:S(2)}) collective-permute-start(s16[24,40,128]{2,1,0:T(8,128)(2,1)} %shard_map.57), channel_id=1, source_target_pairs={{0,0},{48,1},{384,2},{64,3},{112,4},{256,5},{320,6},{368,7},{128,8... | collective-permute-start | bytes 737288 | tf_op jit(solution)/shard_map/ppermute | solution.py:296
  64.5 3.4 %copy-start.3 = (bf16[24,16,256]{2,1,0:T(8,128)(2,1)}, bf16[24,16,256]{2,1,0:T(8,128)(2,1)S(1)}, u32[]{:S(2)}) copy-start(bf16[24,16,256]{2,1,0:T(8,128)(2,1)S(1)} %collective-permute-done.refs_0_) | copy-start | bytes 589828
  64.5 3.3 %collective-permute-start.1 = (bf16[24,16,256]{2,1,0:T(8,128)(2,1)S(1)}, bf16[24,16,256]{2,1,0:T(8,128)(2,1)S(1)}, u32[]{:S(2)}, u32[]{:S(2)}) collective-permute-start(bf16[24,16,256]{2,1,0:T(8,128)(2,1)S(1)} %collective-permute-done.refs_0_), channel_id=1, source_target_pairs={{0,48},{48,0},{96,144},{144,96},{192,240},{240,192},{288,336},{336... | collective-permute-start | bytes 589832 | tf_op jit(solution)/shard_map/ppermute | solution.py:298
  67.8 0.7 copy-start.4
  73.9 0.7 copy-start.2

commit v3 on v2

--- a/solution.py
+++ b/solution.py
@@ -8,7 +8,12 @@
 from jax.sharding import PartitionSpec as P
 
 CHUNK = 16
+GROUP = 8
 TOP = 14
+
+
+def grant(mib):
+    return pltpu.CompilerParams(vmem_limit_bytes=mib * 2**20)
 
 
 def vmem():
@@ -23,49 +28,46 @@
     )
 
 
-def pack(left, right, payload, p):
-    rows, width = left.shape
+def pack(sums, payload, at):
+    group, _, rows, width = sums.shape
     half = rows // 2
-    peak = jnp.max(jnp.maximum(jnp.abs(left), jnp.abs(right)), axis=1, keepdims=True)
+    peak = jnp.max(jnp.max(jnp.abs(sums), axis=1), axis=-1, keepdims=True)
     peak = jnp.maximum(peak, 1.2e-38)
     exponent = jnp.floor(jnp.log2(peak)).astype(jnp.int32)
     first, second = powers(TOP - exponent)
-    for s, part in enumerate((left, right)):
-        scaled = jnp.round((part * first) * second)
+    for s in range(2):
+        scaled = jnp.round((sums[:, s] * first) * second)
         scaled = jnp.minimum(jnp.maximum(scaled, -32767.0), 32767.0)
-        payload[p, s * rows : (s + 1) * rows] = scaled.astype(jnp.int32).astype(jnp.int16)
-    lane = lax.broadcasted_iota(jnp.int32, (half, width), 1)
-    both = jnp.where(lane < width // 2, exponent[:half], exponent[half:])
-    payload[p, 2 * rows : 2 * rows + half] = both.astype(jnp.int16)
-
-
-def unpack(payload, p, rows):
+        scaled = scaled.astype(jnp.int32).astype(jnp.int16)
+        payload[pl.ds(at, group), s * rows : (s + 1) * rows] = scaled
+    lane = lax.broadcasted_iota(jnp.int32, (group, half, width), 2)
+    both = jnp.where(lane < width // 2, exponent[:, :half], exponent[:, half:])
+    payload[pl.ds(at, group), 2 * rows : 2 * rows + half] = both.astype(jnp.int16)
+
+
+def unpack(payload, at, group, rows):
     half = rows // 2
     width = payload.shape[-1]
-    exponent = payload[p, 2 * rows : 2 * rows + half].astype(jnp.int32) - TOP
-    first, second = powers(exponent)
-
-    def spread_out(factor):
-        upper = jnp.broadcast_to(factor[:, :1], (half, width))
-        lower = jnp.broadcast_to(factor[:, width // 2 : width // 2 + 1], (half, width))
-        return jnp.concatenate([upper, lower], axis=0)
-
-    first, second = spread_out(first), spread_out(second)
-    return [
-        (payload[p, s * rows : (s + 1) * rows].astype(jnp.float32) * first) * second
-        for s in range(2)
-    ]
+    exponent = payload[pl.ds(at, group), 2 * rows : 2 * rows + half].astype(jnp.int32)
+    factors = []
+    for factor in powers(exponent - TOP):
+        upper = jnp.broadcast_to(factor[:, :, :1], (group, half, width))
+        lower = factor[:, :, width // 2 : width // 2 + 1]
+        lower = jnp.broadcast_to(lower, (group, half, width))
+        factors.append(jnp.concatenate([upper, lower], axis=1))
+    parts = [payload[pl.ds(at, group), s * rows : (s + 1) * rows] for s in range(2)]
+    return [(part.astype(jnp.float32) * factors[0]) * factors[1] for part in parts]
 
 
 def product_kernel(mirror, meta, sources, targets, *refs):
     if mirror:
-        own, tiles, keep, give, x, acc, held, sems = refs
+        own, tiles, keep, give, x, held, sems, acc = refs
         parts = [own]
     else:
         mine, theirs, tiles, acc, x, held, sems = refs
         parts = [mine, theirs]
-    slots, width = tiles.shape[0], tiles.shape[1]
-    chunks = slots // CHUNK
+    width = tiles.shape[1]
+    chunks = tiles.shape[0] // CHUNK
 
     def copy(step):
         part = pl.ds(step * CHUNK, CHUNK)
@@ -81,12 +83,11 @@
         at += size
     x[at] = jnp.zeros(x.shape[1:], x.dtype)
     acc[...] = jnp.zeros_like(acc)
-    count = meta[0]
 
     def step_body(step, carry):
         copy(step).wait()
 
-        @pl.when(step * CHUNK < count)
+        @pl.when(step * CHUNK < meta[0])
         def _():
             found = []
             for u in range(CHUNK):
@@ -117,35 +118,36 @@
     smem = pl.BlockSpec(memory_space=pltpu.SMEM)
     pieces = segment[0].shape[0] * len(segment)
     vecs = segment[0].shape[1]
-    slots, width = tiles.shape[:2]
+    width = tiles.shape[1]
     scratch = [
         pltpu.VMEM((pieces + 1, 2, vecs, width), jnp.bfloat16),
-        pltpu.VMEM((pieces, 2, vecs, width), jnp.float32),
-        pltpu.VMEM((slots, width, width), jnp.bfloat16),
-        pltpu.SemaphoreType.DMA((slots // CHUNK,)),
+        pltpu.VMEM(tiles.shape, tiles.dtype),
+        pltpu.SemaphoreType.DMA((tiles.shape[0] // CHUNK,)),
     ]
     if mirror:
         shapes = [jax.ShapeDtypeStruct((pieces // 2, 2, vecs, width), jnp.float32)] * 2
         outs = [vmem(), vmem()]
+        scratch.append(pltpu.VMEM((pieces, 2, vecs, width), jnp.float32))
     else:
         shapes = jax.ShapeDtypeStruct((pieces, 2, vecs, width), jnp.float32)
         outs = vmem()
-        del scratch[1]
     return pl.pallas_call(
         functools.partial(product_kernel, mirror),
         out_shape=shapes,
         in_specs=[smem] * 3 + [vmem()] * len(segment) + [pl.BlockSpec(memory_space=pl.ANY)],
         out_specs=outs,
         scratch_shapes=scratch,
+        compiler_params=grant(12),
     )(meta, sources, targets, *segment, tiles)
 
 
 def join_kernel(keep, came, payload):
-    def body(p, carry):
-        pack(keep[p, 0] + came[p, 0], keep[p, 1] + came[p, 1], payload, p)
+    def body(i, carry):
+        part = pl.ds(i * GROUP, GROUP)
+        pack(keep[part] + came[part], payload, i * GROUP)
         return carry
 
-    lax.fori_loop(0, payload.shape[0], body, 0, unroll=4)
+    lax.fori_loop(0, payload.shape[0] // GROUP, body, 0)
 
 
 def join(keep, came):
@@ -155,6 +157,7 @@
         out_shape=jax.ShapeDtypeStruct((pieces, 5 * vecs // 2, width), jnp.int16),
         in_specs=[vmem()] * 2,
         out_specs=vmem(),
+        compiler_params=grant(4),
     )(keep, came)
 
 
@@ -164,12 +167,13 @@
     first, other = side[0] * half, (1 - side[0]) * half
 
     def body(i, carry):
-        left, right = unpack(came, i, vecs)
-        pack(sums[first + i, 0] + left, sums[first + i, 1] + right, payload, first + i)
-        pack(sums[other + i, 0], sums[other + i, 1], payload, other + i)
+        at = i * GROUP
+        added = jnp.stack(unpack(came, at, GROUP, vecs), axis=1)
+        pack(sums[pl.ds(first + at, GROUP)] + added, payload, first + at)
+        pack(sums[pl.ds(other + at, GROUP)], payload, other + at)
         return carry
 
-    lax.fori_loop(0, half, body, 0, unroll=2)
+    lax.fori_loop(0, half // GROUP, body, 0)
 
 
 def merge(side, sums, came):
@@ -179,6 +183,7 @@
         out_shape=jax.ShapeDtypeStruct((pieces, 5 * vecs // 2, width), jnp.int16),
         in_specs=[pl.BlockSpec(memory_space=pltpu.SMEM)] + [vmem()] * 2,
         out_specs=vmem(),
+        compiler_params=grant(4),
     )(side, sums, came)
 
 
@@ -186,11 +191,11 @@
     width = payload.shape[-1]
 
     def body(i, sums):
-        left, right = unpack(payload, i, vecs)
-        return sums[0] + left, sums[1] + right
+        parts = unpack(payload, i * GROUP, GROUP, vecs)
+        return tuple(one + part.sum(axis=0) for one, part in zip(sums, parts))
 
     zero = jnp.zeros((vecs, width), jnp.float32)
-    sums = lax.fori_loop(0, payload.shape[0], body, (zero, zero), unroll=4)
+    sums = lax.fori_loop(0, payload.shape[0] // GROUP, body, (zero, zero))
     for s in range(2):
         out[:, s * width : (s + 1) * width] = sums[s]
 
@@ -201,6 +206,7 @@
         out_shape=jax.ShapeDtypeStruct((vecs, 2 * payload.shape[-1]), jnp.float32),
         in_specs=[vmem()],
         out_specs=vmem(),
+        compiler_params=grant(4),
     )(payload)
 
 
@@ -264,11 +270,19 @@
     return pairs
 
 
+def copies_kernel(array, out):
+    out[...] = jnp.broadcast_to(array[...][None], out.shape)
+
+
 def spread(array, axes):
-    size = lax.axis_size(axes)
-    return lax.all_to_all(
-        jnp.broadcast_to(array[None], (size, *array.shape)), axes, 0, 0, tiled=True
-    )
+    copies = pl.pallas_call(
+        copies_kernel,
+        out_shape=jax.ShapeDtypeStruct((lax.axis_size(axes), *array.shape), array.dtype),
+        in_specs=[vmem()],
+        out_specs=vmem(),
+        compiler_params=grant(2),
+    )(array)
+    return lax.all_to_all(copies, axes, 0, 0, tiled=True)
 
 
 def shards(pairs, vectors, tiles, tile_rows, tile_cols, tile_count):

time: 131 us -> 123 us (0.939)
  Pallas kernels: 19.6 us -> 9.42 us
  waiting for transfers between devices: 21 us -> 24.1 us
    pallas_call x2, Pallas kernels: 10 us -> 6 us  [products(): pl.pallas_call(functools.partial(product_kernel, mirror), out_shape=shape...]
    pallas_call x1, Pallas kernels: 4.31 us -> 0.88 us  [merge(): pl.pallas_call(merge_kernel, out_shape=jax.ShapeDtypeStruct((pieces, 5 *...]
    ppermute x1, waiting for transfers between devices: 0.01 us -> 2.48 us  [shards(): mine = lax.ppermute(mine, axes, pairs)]
    unnamed x10 -> x8, local copies, waits for them, and re-layouts: 2.85 us -> 5.08 us
    pallas_call x1, Pallas kernels: 2.52 us -> 0.43 us  [join(): pl.pallas_call(join_kernel, out_shape=jax.ShapeDtypeStruct((pieces, 5 * v...]
    pallas_call x1, Pallas kernels: 2.8 us -> 1.34 us  [total(): pl.pallas_call(functools.partial(total_kernel, vecs), out_shape=jax.Shape...]
    broadcast_in_dim x1 -> x0, local copies, waits for them, and re-layouts: 1.46 us -> none  [spread(): jnp.broadcast_to(array[None], (size, *array.shape))]
  transfers between devices with their start and end apart: 5 -> 5, of which waited for: 2 -> 3; matrix products, arithmetic and copies ran while one was open for 2% -> 1% of each run, Pallas kernels for 6% -> 3%
where the time goes in v3:
time: 123 us
  blocking collectives  49.1 us (40%)
  starting transfers between devices  33.7 us (27%)
  waiting for transfers between devices  24.1 us (20%)
  Pallas kernels  9.42 us (8%)
  local copies, waits for them, and re-layouts  5.1 us (4%)
    all_to_all x1, blocking collectives, shards(): plain = lax.all_to_all(plain, 'col', 0, 0, tiled=True)  49.1 us
    all_to_all x1, waiting for transfers between devices, spread(): return lax.all_to_all(copies, axes, 0, 0, tiled=True)  20.2 us
    all_to_all x1, starting transfers between devices, spread(): return lax.all_to_all(copies, axes, 0, 0, tiled=True)  18.9 us
    ppermute x1, starting transfers between devices, shards(): sums = lax.ppermute(sums, axes, [(taker, giver) for giver, taker in pairs])  8.15 us
    pallas_call x2, Pallas kernels, products(): pl.pallas_call(functools.partial(product_kernel, mirror), out_shape=shape...  6 us
    unnamed x8, local copies, waits for them, and re-layouts  5.08 us
    ppermute x1, starting transfers between devices, shards(): mine = lax.ppermute(mine, axes, pairs)  2.81 us
    ppermute x1, waiting for transfers between devices, shards(): mine = lax.ppermute(mine, axes, pairs)  2.48 us
  transfers between devices with their start and end apart: 5, of which 3 were waited for; matrix products, arithmetic and copies ran while one was open for 1% of the time, Pallas kernels for 3%

profile of v3, /device:TPU:6, one launch (start us, length us, event | category | flops | bytes accessed | tf_op | source)
XLA Modules:
  0.0 122.8 jit_solution(18337855459639979101)
XLA Ops:
  0.0 0.0 copy-start.2
  0.0 0.7 copy-done.2
  0.7 0.0 copy-start.3
  0.7 0.8 shard_map.55
  1.5 18.9 %all-to-all-start = ((bf16[48,16,256]{2,1,0:T(8,128)(2,1)}), bf16[48,16,256]{2,1,0:T(8,128)(2,1)S(1)}, u32[]{:S(2)}, u32[]{:S(2)}) async-start(bf16[48,16,256]{2,1,0:T(8,128)(2,1)} %shard_map.55), calls=%async_computation | async-start | bytes 786432 | tf_op jit(solution)/shard_map/all_to_all | solution.py:285
  21.0 0.7 compare_select_fusion
  21.7 20.2 %all-to-all-done.refs_0_ = bf16[48,16,256]{2,1,0:T(8,128)(2,1)S(1)} async-done(((bf16[48,16,256]{2,1,0:T(8,128)(2,1)}), bf16[48,16,256]{2,1,0:T(8,128)(2,1)S(1)}, u32[]{:S(2)}, u32[]{:S(2)}) %all-to-all-start) | async-done | bytes 393248 | tf_op jit(solution)/shard_map/all_to_all | solution.py:285
  41.9 0.0 copy-start
  41.9 2.2 %copy-done = bf16[128,128,128]{2,1,0:T(8,128)(2,1)S(1)} copy-done((bf16[128,128,128]{2,1,0:T(8,128)(2,1)S(1)}, bf16[128,128,128]{2,1,0:T(8,128)(2,1)}, u32[]{:S(2)}) %copy-start) | copy-done | bytes 4194328
  44.1 2.6 %shard_map.57 = (f32[24,2,16,128]{3,2,1,0:T(8,128)S(1)}, f32[24,2,16,128]{3,2,1,0:T(8,128)S(1)}) custom-call(s32[1]{0:T(128)} %copy.6.meta, s32[128]{0:T(128)S(1)} %get-tuple-element.11.sources, s32[128]{0:T(128)S(1)} %get-tuple-element.10.targets, bf16[48,16,256]{2,1,0:T(8,128)(2,1)S(1)} %all-to-all-done.refs_0_, bf16[128,128,128]{2,1,0:T(8,128)(2,1)S(1)} %copy-done), custom_call_target="tpu_custom_call" | custom-call | tf_op jit(solution)/shard_map/pallas_call | solution.py:134
  46.8 1.9 %collective-permute-start.2 = (f32[24,2,16,128]{3,2,1,0:T(8,128)S(1)}, f32[24,2,16,128]{3,2,1,0:T(8,128)S(1)}, u32[]{:S(2)}, u32[]{:S(2)}) collective-permute-start(f32[24,2,16,128]{3,2,1,0:T(8,128)S(1)} %get-tuple-element.8), channel_id=1, source_target_pairs={{0,48},{48,0},{96,144},{144,96},{192,240},{240,192},{288,336},{336... | collective-permute-start | bytes 1179656 | tf_op jit(solution)/shard_map/ppermute | solution.py:308
  48.8 2.8 %collective-permute-start = (bf16[24,16,256]{2,1,0:T(8,128)(2,1)S(1)}, bf16[24,16,256]{2,1,0:T(8,128)(2,1)S(1)}, u32[]{:S(2)}, u32[]{:S(2)}) collective-permute-start(bf16[24,16,256]{2,1,0:T(8,128)(2,1)S(1)} %constant_dynamic-slice_fusion), channel_id=1, source_target_pairs={{0,0},{1,48},{2,384},{3,64},{4,112},{5,256},{6,320},{7,368},{8,128... | collective-permute-start | bytes 589832 | tf_op jit(solution)/shard_map/ppermute | solution.py:306
  51.6 0.0 collective-permute-done.2.came
  51.6 0.4 shard_map.58
  52.0 8.2 %collective-permute-start.3 = (s16[24,40,128]{2,1,0:T(8,128)(2,1)S(1)}, s16[24,40,128]{2,1,0:T(8,128)(2,1)S(1)}, u32[]{:S(2)}, u32[]{:S(2)}) collective-permute-start(s16[24,40,128]{2,1,0:T(8,128)(2,1)S(1)} %shard_map.58), channel_id=1, source_target_pairs={{0,0},{48,1},{384,2},{64,3},{112,4},{256,5},{320,6},{368,7},{128,8... | collective-permute-start | bytes 737288 | tf_op jit(solution)/shard_map/ppermute | solution.py:310
  60.2 2.5 %collective-permute-done.refs_0_ = bf16[24,16,256]{2,1,0:T(8,128)(2,1)S(1)} collective-permute-done((bf16[24,16,256]{2,1,0:T(8,128)(2,1)S(1)}, bf16[24,16,256]{2,1,0:T(8,128)(2,1)S(1)}, u32[]{:S(2)}, u32[]{:S(2)}) %collective-permute-start) | collective-permute-done | bytes 196640 | tf_op jit(solution)/shard_map/ppermute | solution.py:306
  62.7 1.9 %collective-permute-start.1 = (bf16[24,16,256]{2,1,0:T(8,128)(2,1)S(1)}, bf16[24,16,256]{2,1,0:T(8,128)(2,1)S(1)}, u32[]{:S(2)}, u32[]{:S(2)}) collective-permute-start(bf16[24,16,256]{2,1,0:T(8,128)(2,1)S(1)} %collective-permute-done.refs_0_), channel_id=1, source_target_pairs={{0,48},{48,0},{96,144},{144,96},{192,240},{240,192},{288,336},{336... | collective-permute-start | bytes 589832 | tf_op jit(solution)/shard_map/ppermute | solution.py:312
  64.6 1.4 %collective-permute-done.1.refs_1_ = bf16[24,16,256]{2,1,0:T(8,128)(2,1)S(1)} collective-permute-done((bf16[24,16,256]{2,1,0:T(8,128)(2,1)S(1)}, bf16[24,16,256]{2,1,0:T(8,128)(2,1)S(1)}, u32[]{:S(2)}, u32[]{:S(2)}) %collective-permute-start.1) | collective-permute-done | bytes 196640 | tf_op jit(solution)/shard_map/ppermute | solution.py:312
  66.0 0.0 copy-done.3
  66.0 0.0 copy-start.1
  66.0 2.2 %copy-done.1 = bf16[128,128,128]{2,1,0:T(8,128)(2,1)S(1)} copy-done((bf16[128,128,128]{2,1,0:T(8,128)(2,1)S(1)}, bf16[128,128,128]{2,1,0:T(8,128)(2,1)}, u32[]{:S(2)}) %copy-start.1) | copy-done | bytes 4194328
  68.2 3.4 %shard_map.56.sums = f32[48,2,16,128]{3,2,1,0:T(8,128)S(1)} custom-call(s32[1]{0:T(128)} %copy.6.meta, s32[128]{0:T(128)S(1)} %get-tuple-element.9.sources, s32[128]{0:T(128)S(1)} %copy-done.3, bf16[24,16,256]{2,1,0:T(8,128)(2,1)S(1)} %collective-permute-done.refs_0_, bf16[24,16,256]{2,1,0:T(8,128)(2,1)S(1)} %collective-permute-done.1.refs_1_, ...), custom_call_target="tpu_custom_call" | custom-call | tf_op jit(solution)/shard_map/pallas_call | solution.py:134
  71.5 0.0 collective-permute-done.3.came
  71.5 0.9 shard_map.59
  72.4 49.1 %all_to_all.10.payload = s16[48,40,128]{2,1,0:T(8,128)(2,1)S(1)} all-to-all(s16[48,40,128]{2,1,0:T(8,128)(2,1)S(1)} %shard_map.59), channel_id=1, replica_groups=mesh['row'=16,'col'=48] {'col'}, dimensions={0} | all-to-all | bytes 983040 | tf_op jit(solution)/shard_map/all_to_all | solution.py:315
  121.5 1.3 %shard_map.60 = f32[16,256]{1,0:T(8,128)} custom-call(s16[48,40,128]{2,1,0:T(8,128)(2,1)S(1)} %all_to_all.10.payload), custom_call_target="tpu_custom_call" | custom-call | tf_op jit(solution)/shard_map/pallas_call | solution.py:204
  (1 shorter events, 0.0 us)
Async XLA Ops:
  0.0 0.7 copy-start.2
  0.7 65.3 %copy-start.3 = (s32[128]{0:T(128)S(1)}, s32[128]{0:T(128)}, u32[]{:S(2)}) copy-start(s32[128]{0:T(128)} %targets.1) | copy-start | bytes 1540
  1.5 40.5 %all-to-all-start = ((bf16[48,16,256]{2,1,0:T(8,128)(2,1)}), bf16[48,16,256]{2,1,0:T(8,128)(2,1)S(1)}, u32[]{:S(2)}, u32[]{:S(2)}) async-start(bf16[48,16,256]{2,1,0:T(8,128)(2,1)} %shard_map.55), calls=%async_computation | async-start | bytes 786432 | tf_op jit(solution)/shard_map/all_to_all | solution.py:285
  41.9 2.2 %copy-start = (bf16[128,128,128]{2,1,0:T(8,128)(2,1)S(1)}, bf16[128,128,128]{2,1,0:T(8,128)(2,1)}, u32[]{:S(2)}) copy-start(bf16[128,128,128]{2,1,0:T(8,128)(2,1)} %refs_1_.1) | copy-start | bytes 12582916
  46.8 4.8 %collective-permute-start.2 = (f32[24,2,16,128]{3,2,1,0:T(8,128)S(1)}, f32[24,2,16,128]{3,2,1,0:T(8,128)S(1)}, u32[]{:S(2)}, u32[]{:S(2)}) collective-permute-start(f32[24,2,16,128]{3,2,1,0:T(8,128)S(1)} %get-tuple-element.8), channel_id=1, source_target_pairs={{0,48},{48,0},{96,144},{144,96},{192,240},{240,192},{288,336},{336... | collective-permute-start | bytes 1179656 | tf_op jit(solution)/shard_map/ppermute | solution.py:308
  48.8 13.9 %collective-permute-start = (bf16[24,16,256]{2,1,0:T(8,128)(2,1)S(1)}, bf16[24,16,256]{2,1,0:T(8,128)(2,1)S(1)}, u32[]{:S(2)}, u32[]{:S(2)}) collective-permute-start(bf16[24,16,256]{2,1,0:T(8,128)(2,1)S(1)} %constant_dynamic-slice_fusion), channel_id=1, source_target_pairs={{0,0},{1,48},{2,384},{3,64},{4,112},{5,256},{6,320},{7,368},{8,128... | collective-permute-start | bytes 589832 | tf_op jit(solution)/shard_map/ppermute | solution.py:306
  52.0 19.5 %collective-permute-start.3 = (s16[24,40,128]{2,1,0:T(8,128)(2,1)S(1)}, s16[24,40,128]{2,1,0:T(8,128)(2,1)S(1)}, u32[]{:S(2)}, u32[]{:S(2)}) collective-permute-start(s16[24,40,128]{2,1,0:T(8,128)(2,1)S(1)} %shard_map.58), channel_id=1, source_target_pairs={{0,0},{48,1},{384,2},{64,3},{112,4},{256,5},{320,6},{368,7},{128,8... | collective-permute-start | bytes 737288 | tf_op jit(solution)/shard_map/ppermute | solution.py:310
  62.7 3.3 %collective-permute-start.1 = (bf16[24,16,256]{2,1,0:T(8,128)(2,1)S(1)}, bf16[24,16,256]{2,1,0:T(8,128)(2,1)S(1)}, u32[]{:S(2)}, u32[]{:S(2)}) collective-permute-start(bf16[24,16,256]{2,1,0:T(8,128)(2,1)S(1)} %collective-permute-done.refs_0_), channel_id=1, source_target_pairs={{0,48},{48,0},{96,144},{144,96},{192,240},{240,192},{288,336},{336... | collective-permute-start | bytes 589832 | tf_op jit(solution)/shard_map/ppermute | solution.py:312
  66.0 2.2 %copy-start.1 = (bf16[128,128,128]{2,1,0:T(8,128)(2,1)S(1)}, bf16[128,128,128]{2,1,0:T(8,128)(2,1)}, u32[]{:S(2)}) copy-start(bf16[128,128,128]{2,1,0:T(8,128)(2,1)} %refs_1_.1) | copy-start | bytes 12582916

commit v4 on v3

--- a/solution.py
+++ b/solution.py
@@ -134,7 +134,7 @@
     return pl.pallas_call(
         functools.partial(product_kernel, mirror),
         out_shape=shapes,
-        in_specs=[smem] * 3 + [vmem()] * len(segment) + [pl.BlockSpec(memory_space=pl.ANY)],
+        in_specs=[smem] * 3 + [vmem()] * len(segment) + [pl.BlockSpec(memory_space=pltpu.HBM)],
         out_specs=outs,
         scratch_shapes=scratch,
         compiler_params=grant(12),
@@ -277,7 +277,7 @@
 def spread(array, axes):
     copies = pl.pallas_call(
         copies_kernel,
-        out_shape=jax.ShapeDtypeStruct((lax.axis_size(axes), *array.shape), array.dtype),
+        out_shape=pltpu.VMEM((lax.axis_size(axes), *array.shape), array.dtype),
         in_specs=[vmem()],
         out_specs=vmem(),
         compiler_params=grant(2),
@@ -301,6 +301,7 @@
     mirror_source = jnp.where(mirrored, tile_rows, nothing)
     plain_source = jnp.where(live, col_place, nothing)
 
+    tiles = pltpu.with_memory_space_constraint(tiles, pltpu.HBM)
     own = spread(vectors, "col")
     mine = lax.dynamic_slice_in_dim(own, side * pieces, pieces, 0)
     mine = lax.ppermute(mine, axes, pairs)

time: 123 us -> 120 us (0.976)
  local copies, waits for them, and re-layouts: 5.1 us -> 0.72 us
  Pallas kernels: 9.42 us -> 10.7 us
    unnamed x8 -> x4, local copies, waits for them, and re-layouts: 5.08 us -> 0.7 us
    pallas_call x2, Pallas kernels: 6 us -> 7.32 us  [products(): pl.pallas_call(functools.partial(product_kernel, mirror), out_shape=shape...]
  transfers between devices with their start and end apart: 5 -> 5, of which waited for: 3 -> 3; matrix products, arithmetic and copies ran while one was open for 1% -> 1% of each run, Pallas kernels for 3% -> 4%
where the time goes in v4:
time: 120 us
  blocking collectives  49.1 us (41%)
  starting transfers between devices  33.7 us (28%)
  waiting for transfers between devices  24.1 us (20%)
  Pallas kernels  10.7 us (9%)
    all_to_all x1, blocking collectives, shards(): plain = lax.all_to_all(plain, 'col', 0, 0, tiled=True)  49.1 us
    all_to_all x1, waiting for transfers between devices, spread(): return lax.all_to_all(copies, axes, 0, 0, tiled=True)  20.2 us
    all_to_all x1, starting transfers between devices, spread(): return lax.all_to_all(copies, axes, 0, 0, tiled=True)  18.9 us
    ppermute x1, starting transfers between devices, shards(): sums = lax.ppermute(sums, axes, [(taker, giver) for giver, taker in pairs])  8.15 us
    pallas_call x2, Pallas kernels, products(): pl.pallas_call(functools.partial(product_kernel, mirror), out_shape=shape...  7.32 us
    ppermute x1, starting transfers between devices, shards(): mine = lax.ppermute(mine, axes, pairs)  2.81 us
    ppermute x1, waiting for transfers between devices, shards(): mine = lax.ppermute(mine, axes, pairs)  2.48 us
  transfers between devices with their start and end apart: 5, of which 3 were waited for; matrix products, arithmetic and copies ran while one was open for 1% of the time, Pallas kernels for 4%

profile of v4, /device:TPU:6, one launch (start us, length us, event | category | flops | bytes accessed | tf_op | source)
XLA Modules:
  0.0 119.8 jit_solution(12048196794979746780)
XLA Ops:
  0.0 0.0 copy-start
  0.0 0.7 copy-done
  0.7 0.0 copy-start.1
  0.7 0.8 shard_map.55
  1.5 18.9 %all-to-all-start = ((bf16[48,16,256]{2,1,0:T(8,128)(2,1)}), bf16[48,16,256]{2,1,0:T(8,128)(2,1)S(1)}, u32[]{:S(2)}, u32[]{:S(2)}) async-start(bf16[48,16,256]{2,1,0:T(8,128)(2,1)} %shard_map.55), calls=%async_computation | async-start | bytes 786432 | tf_op jit(solution)/shard_map/all_to_all | solution.py:285
  21.0 0.7 compare_select_fusion
  21.7 20.2 %all-to-all-done.refs_0_ = bf16[48,16,256]{2,1,0:T(8,128)(2,1)S(1)} async-done(((bf16[48,16,256]{2,1,0:T(8,128)(2,1)}), bf16[48,16,256]{2,1,0:T(8,128)(2,1)S(1)}, u32[]{:S(2)}, u32[]{:S(2)}) %all-to-all-start) | async-done | bytes 393248 | tf_op jit(solution)/shard_map/all_to_all | solution.py:285
  41.9 3.3 %shard_map.57 = (f32[24,2,16,128]{3,2,1,0:T(8,128)S(1)}, f32[24,2,16,128]{3,2,1,0:T(8,128)S(1)}) custom-call(s32[1]{0:T(128)} %copy.6.meta, s32[128]{0:T(128)S(1)} %get-tuple-element.11.sources, s32[128]{0:T(128)S(1)} %get-tuple-element.10.targets, bf16[48,16,256]{2,1,0:T(8,128)(2,1)S(1)} %all-to-all-done.refs_0_, bf16[128,128,128]{2,1,0:T(8,128)(2,1)} %refs_1_.1), custom_call_target="tpu_custom_call" | custom-call | tf_op jit(solution)/shard_map/pallas_call | solution.py:134
  45.2 1.9 %collective-permute-start.2 = (f32[24,2,16,128]{3,2,1,0:T(8,128)S(1)}, f32[24,2,16,128]{3,2,1,0:T(8,128)S(1)}, u32[]{:S(2)}, u32[]{:S(2)}) collective-permute-start(f32[24,2,16,128]{3,2,1,0:T(8,128)S(1)} %get-tuple-element.8), channel_id=1, source_target_pairs={{0,48},{48,0},{96,144},{144,96},{192,240},{240,192},{288,336},{336... | collective-permute-start | bytes 1179656 | tf_op jit(solution)/shard_map/ppermute | solution.py:309
  47.2 2.8 %collective-permute-start = (bf16[24,16,256]{2,1,0:T(8,128)(2,1)S(1)}, bf16[24,16,256]{2,1,0:T(8,128)(2,1)S(1)}, u32[]{:S(2)}, u32[]{:S(2)}) collective-permute-start(bf16[24,16,256]{2,1,0:T(8,128)(2,1)S(1)} %constant_dynamic-slice_fusion), channel_id=1, source_target_pairs={{0,0},{1,48},{2,384},{3,64},{4,112},{5,256},{6,320},{7,368},{8,128... | collective-permute-start | bytes 589832 | tf_op jit(solution)/shard_map/ppermute | solution.py:307
  50.0 0.0 collective-permute-done.2.came
  50.0 0.4 shard_map.58
  50.5 8.2 %collective-permute-start.3 = (s16[24,40,128]{2,1,0:T(8,128)(2,1)S(1)}, s16[24,40,128]{2,1,0:T(8,128)(2,1)S(1)}, u32[]{:S(2)}, u32[]{:S(2)}) collective-permute-start(s16[24,40,128]{2,1,0:T(8,128)(2,1)S(1)} %shard_map.58), channel_id=1, source_target_pairs={{0,0},{48,1},{384,2},{64,3},{112,4},{256,5},{320,6},{368,7},{128,8... | collective-permute-start | bytes 737288 | tf_op jit(solution)/shard_map/ppermute | solution.py:311
  58.6 2.5 %collective-permute-done.refs_0_ = bf16[24,16,256]{2,1,0:T(8,128)(2,1)S(1)} collective-permute-done((bf16[24,16,256]{2,1,0:T(8,128)(2,1)S(1)}, bf16[24,16,256]{2,1,0:T(8,128)(2,1)S(1)}, u32[]{:S(2)}, u32[]{:S(2)}) %collective-permute-start) | collective-permute-done | bytes 196640 | tf_op jit(solution)/shard_map/ppermute | solution.py:307
  61.1 1.9 %collective-permute-start.1 = (bf16[24,16,256]{2,1,0:T(8,128)(2,1)S(1)}, bf16[24,16,256]{2,1,0:T(8,128)(2,1)S(1)}, u32[]{:S(2)}, u32[]{:S(2)}) collective-permute-start(bf16[24,16,256]{2,1,0:T(8,128)(2,1)S(1)} %collective-permute-done.refs_0_), channel_id=1, source_target_pairs={{0,48},{48,0},{96,144},{144,96},{192,240},{240,192},{288,336},{336... | collective-permute-start | bytes 589832 | tf_op jit(solution)/shard_map/ppermute | solution.py:313
  63.0 1.4 %collective-permute-done.1.refs_1_ = bf16[24,16,256]{2,1,0:T(8,128)(2,1)S(1)} collective-permute-done((bf16[24,16,256]{2,1,0:T(8,128)(2,1)S(1)}, bf16[24,16,256]{2,1,0:T(8,128)(2,1)S(1)}, u32[]{:S(2)}, u32[]{:S(2)}) %collective-permute-start.1) | collective-permute-done | bytes 196640 | tf_op jit(solution)/shard_map/ppermute | solution.py:313
  64.4 0.0 copy-done.1
  64.4 4.0 %shard_map.56.sums = f32[48,2,16,128]{3,2,1,0:T(8,128)S(1)} custom-call(s32[1]{0:T(128)} %copy.6.meta, s32[128]{0:T(128)S(1)} %get-tuple-element.9.sources, s32[128]{0:T(128)S(1)} %copy-done.1, bf16[24,16,256]{2,1,0:T(8,128)(2,1)S(1)} %collective-permute-done.refs_0_, bf16[24,16,256]{2,1,0:T(8,128)(2,1)S(1)} %collective-permute-done.1.refs_1_, ...), custom_call_target="tpu_custom_call" | custom-call | tf_op jit(solution)/shard_map/pallas_call | solution.py:134
  68.5 0.0 collective-permute-done.3.came
  68.5 0.9 shard_map.59
  69.4 49.1 %all_to_all.10.payload = s16[48,40,128]{2,1,0:T(8,128)(2,1)S(1)} all-to-all(s16[48,40,128]{2,1,0:T(8,128)(2,1)S(1)} %shard_map.59), channel_id=1, replica_groups=mesh['row'=16,'col'=48] {'col'}, dimensions={0} | all-to-all | bytes 983040 | tf_op jit(solution)/shard_map/all_to_all | solution.py:316
  118.4 1.3 %shard_map.60 = f32[16,256]{1,0:T(8,128)} custom-call(s16[48,40,128]{2,1,0:T(8,128)(2,1)S(1)} %all_to_all.10.payload), custom_call_target="tpu_custom_call" | custom-call | tf_op jit(solution)/shard_map/pallas_call | solution.py:204
  (1 shorter events, 0.0 us)
Async XLA Ops:
  0.0 0.7 copy-start
  0.7 63.8 %copy-start.1 = (s32[128]{0:T(128)S(1)}, s32[128]{0:T(128)}, u32[]{:S(2)}) copy-start(s32[128]{0:T(128)} %targets.1) | copy-start | bytes 1540
  1.5 40.5 %all-to-all-start = ((bf16[48,16,256]{2,1,0:T(8,128)(2,1)}), bf16[48,16,256]{2,1,0:T(8,128)(2,1)S(1)}, u32[]{:S(2)}, u32[]{:S(2)}) async-start(bf16[48,16,256]{2,1,0:T(8,128)(2,1)} %shard_map.55), calls=%async_computation | async-start | bytes 786432 | tf_op jit(solution)/shard_map/all_to_all | solution.py:285
  45.2 4.8 %collective-permute-start.2 = (f32[24,2,16,128]{3,2,1,0:T(8,128)S(1)}, f32[24,2,16,128]{3,2,1,0:T(8,128)S(1)}, u32[]{:S(2)}, u32[]{:S(2)}) collective-permute-start(f32[24,2,16,128]{3,2,1,0:T(8,128)S(1)} %get-tuple-element.8), channel_id=1, source_target_pairs={{0,48},{48,0},{96,144},{144,96},{192,240},{240,192},{288,336},{336... | collective-permute-start | bytes 1179656 | tf_op jit(solution)/shard_map/ppermute | solution.py:309
  47.2 13.9 %collective-permute-start = (bf16[24,16,256]{2,1,0:T(8,128)(2,1)S(1)}, bf16[24,16,256]{2,1,0:T(8,128)(2,1)S(1)}, u32[]{:S(2)}, u32[]{:S(2)}) collective-permute-start(bf16[24,16,256]{2,1,0:T(8,128)(2,1)S(1)} %constant_dynamic-slice_fusion), channel_id=1, source_target_pairs={{0,0},{1,48},{2,384},{3,64},{4,112},{5,256},{6,320},{7,368},{8,128... | collective-permute-start | bytes 589832 | tf_op jit(solution)/shard_map/ppermute | solution.py:307
  50.5 18.0 %collective-permute-start.3 = (s16[24,40,128]{2,1,0:T(8,128)(2,1)S(1)}, s16[24,40,128]{2,1,0:T(8,128)(2,1)S(1)}, u32[]{:S(2)}, u32[]{:S(2)}) collective-permute-start(s16[24,40,128]{2,1,0:T(8,128)(2,1)S(1)} %shard_map.58), channel_id=1, source_target_pairs={{0,0},{48,1},{384,2},{64,3},{112,4},{256,5},{320,6},{368,7},{128,8... | collective-permute-start | bytes 737288 | tf_op jit(solution)/shard_map/ppermute | solution.py:311
  61.1 3.3 %collective-permute-start.1 = (bf16[24,16,256]{2,1,0:T(8,128)(2,1)S(1)}, bf16[24,16,256]{2,1,0:T(8,128)(2,1)S(1)}, u32[]{:S(2)}, u32[]{:S(2)}) collective-permute-start(bf16[24,16,256]{2,1,0:T(8,128)(2,1)S(1)} %collective-permute-done.refs_0_), channel_id=1, source_target_pairs={{0,48},{48,0},{96,144},{144,96},{192,240},{240,192},{288,336},{336... | collective-permute-start | bytes 589832 | tf_op jit(solution)/shard_map/ppermute | solution.py:313
